TPU v7x, 512 devices: a whole 4x4x16 slice. The times are simulated.
512 devices in a mesh: expert: 128 (over y, x, z_lo), hidden: 4 (over z_hi, core).
Axes of the slice: x: 4, y: 4, z: 16 (z_hi: 2, z_lo: 8; z = z_hi * 8 + z_lo), core: 2. Of those that a mesh axis runs over, the one named last changes fastest.
Arguments:
- tokens: bfloat16 [256, 196, 1024], P('expert', None, 'hidden'), may hold values from -64 to 64
- slot_params: bfloat16 [1024, 128], P('hidden'), may hold values from -0.4 to 0.4
- weight_in: bfloat16 [128, 1024, 4096], P('expert', None, 'hidden'), may hold values from -0.1875 to 0.1875
- bias_in: bfloat16 [128, 4096], P('expert', 'hidden'), may hold values from -3 to 3
- weight_out: bfloat16 [128, 4096, 1024], P('expert', 'hidden'), may hold values from -0.09375 to 0.09375
- bias_out: bfloat16 [128, 1024], P('expert', 'hidden'), may hold values from -3 to 3
- cotangent: bfloat16 [256, 196, 1024], P('expert', None, 'hidden'), may hold values from -1.5 to 1.5
Outputs:
- mixed: bfloat16 [256, 196, 1024], P('expert', None, 'hidden')
- token_grad: bfloat16 [256, 196, 1024], P('expert', None, 'hidden')
- zloss: float32 [256, 196], P('expert')
All inputs are finite; a program needn't handle non-finite values.
Results may differ from a plain program's by a relative error of at most 0.015.
Values may be sent and summed in bfloat16 or wider, within the bound.
A program may use at most 64 MiB of HBM per device.

v0:
```python
import jax
import jax.numpy as jnp
from jax import lax
from jax.sharding import PartitionSpec as P

loss_weight = 0.1


def sent_to_all(x, axis):
    copies = jnp.broadcast_to(x, (lax.axis_size(axis), *x.shape))
    return lax.all_to_all(copies, axis, split_axis=0, concat_axis=0, tiled=True)


def of_everyone(x, axis):
    everything = sent_to_all(x, axis)
    return jnp.sum(everything, axis=0)


def in_order(tiles, dim):
    tiles = jnp.moveaxis(tiles, 0, dim)
    lengths = tiles.shape
    return tiles.reshape(*lengths[:dim], lengths[dim] * lengths[dim + 1], *lengths[dim + 2 :])


def gathered_copies(x, axis, dim):
    return in_order(sent_to_all(x, axis), dim)


def split_up(x, dim, peers):
    lengths = x.shape
    tiles = x.reshape(*lengths[:dim], peers, lengths[dim] // peers, *lengths[dim + 1 :])
    return jnp.moveaxis(tiles, dim, 0)


def sent_and_summed(x, axis, dim):
    peers = lax.axis_size(axis)
    tiles = lax.all_to_all(split_up(x, dim, peers), axis, 0, 0, tiled=True)
    return jnp.sum(tiles.astype(jnp.float32), axis=0)


def taken_together(x, axis):
    everything = sent_to_all(x, axis)
    return jnp.sum(everything.astype(jnp.float32), axis=0)


def gelu_parts(value):
    factor = 0.7978845608028654
    inner = factor * (value + 0.044715 * value * value * value)
    slope_tanh = jnp.tanh(inner)
    result = 0.5 * value * (1.0 + slope_tanh)
    slope = 0.5 * (1.0 + slope_tanh) + 0.5 * value * (1.0 - slope_tanh * slope_tanh) * factor * (
        1.0 + 3.0 * 0.044715 * value * value
    )
    return (result, slope)


def per_device(tokens, slot_params, weight_in, bias_in, weight_out, bias_out, cotangent):
    images_dev = tokens.shape[0]
    groups = lax.axis_size("expert")
    local_experts = weight_in.shape[0]
    quarter = tokens.shape[2]
    partial_value = jnp.einsum(
        "itd,ds->its", tokens, slot_params, preferred_element_type=jnp.float32
    )
    logits = of_everyone(partial_value, "hidden")
    dispatch = jax.nn.softmax(logits, axis=1)
    combine = jax.nn.softmax(logits, axis=2)
    log_total = jax.nn.logsumexp(logits, axis=2)
    zloss = loss_weight * log_total * log_total
    dispatch_low = dispatch.astype(jnp.bfloat16)
    combine_low = combine.astype(jnp.bfloat16)
    slot_in = jnp.einsum(
        "its,itd->isd", dispatch_low, tokens, preferred_element_type=jnp.float32
    ).astype(jnp.bfloat16)
    arrived = lax.all_to_all(slot_in, "expert", split_axis=1, concat_axis=0, tiled=True)
    pre_act = jnp.einsum(
        "ren,enf->ref",
        gathered_copies(arrived, "hidden", 2),
        weight_in,
        preferred_element_type=jnp.float32,
    )
    pre_act = pre_act + bias_in.astype(jnp.float32)[None]
    activated, slope = gelu_parts(pre_act)
    act_low = activated.astype(jnp.bfloat16)
    out_terms = jnp.einsum("ref,efd->red", act_low, weight_out, preferred_element_type=jnp.float32)
    expert_out = sent_and_summed(out_terms.astype(jnp.bfloat16), "hidden", 2)
    expert_low = (expert_out + bias_out.astype(jnp.float32)[None]).astype(jnp.bfloat16)
    slot_out = lax.all_to_all(
        expert_low.reshape(groups, images_dev, local_experts, quarter),
        "expert",
        split_axis=0,
        concat_axis=2,
        tiled=True,
    )
    slot_out = slot_out.reshape(images_dev, groups * local_experts, quarter)
    mixed = jnp.einsum(
        "its,isd->itd", combine_low, slot_out, preferred_element_type=jnp.float32
    ).astype(jnp.bfloat16)
    combine_part = jnp.einsum(
        "itd,isd->its", cotangent, slot_out, preferred_element_type=jnp.float32
    )
    out_grad = jnp.einsum(
        "its,itd->isd", combine_low, cotangent, preferred_element_type=jnp.float32
    ).astype(jnp.bfloat16)
    grad_arrived = lax.all_to_all(out_grad, "expert", split_axis=1, concat_axis=0, tiled=True)
    hidden_grad = jnp.einsum(
        "ren,efn->ref",
        gathered_copies(grad_arrived, "hidden", 2),
        weight_out,
        preferred_element_type=jnp.float32,
    )
    pre_grad = (hidden_grad * slope).astype(jnp.bfloat16)
    in_terms = jnp.einsum("ref,ekf->rek", pre_grad, weight_in, preferred_element_type=jnp.float32)
    slot_grad = sent_and_summed(in_terms.astype(jnp.bfloat16), "hidden", 2).astype(jnp.bfloat16)
    in_grad = lax.all_to_all(
        slot_grad.reshape(groups, images_dev, local_experts, quarter),
        "expert",
        split_axis=0,
        concat_axis=2,
        tiled=True,
    )
    in_grad = in_grad.reshape(images_dev, groups * local_experts, quarter)
    dispatch_part = jnp.einsum("itd,isd->its", tokens, in_grad, preferred_element_type=jnp.float32)
    combine_grad, dispatch_grad = (
        taken_together(combine_part.astype(jnp.bfloat16), "hidden").astype(jnp.float32),
        taken_together(dispatch_part.astype(jnp.bfloat16), "hidden").astype(jnp.float32),
    )
    from_combine = (
        combine * (combine_grad - jnp.sum(combine * combine_grad, axis=2, keepdims=True))
        + 2.0 * loss_weight * log_total[:, :, None] * combine
    )
    from_dispatch = dispatch * (
        dispatch_grad - jnp.sum(dispatch * dispatch_grad, axis=1, keepdims=True)
    )
    logit_low = (from_combine + from_dispatch).astype(jnp.bfloat16)
    token_grad = jnp.einsum(
        "its,ds->itd", logit_low, slot_params, preferred_element_type=jnp.float32
    )
    token_grad = token_grad + jnp.einsum(
        "its,isd->itd", dispatch_low, in_grad, preferred_element_type=jnp.float32
    )
    return (mixed, token_grad.astype(jnp.bfloat16), zloss)


def solution(mesh):
    return jax.shard_map(
        per_device,
        mesh=mesh,
        in_specs=(
            P("expert", None, "hidden"),
            P("hidden", None),
            P("expert", None, "hidden"),
            P("expert", "hidden"),
            P("expert", "hidden", None),
            P("expert", "hidden"),
            P("expert", None, "hidden"),
        ),
        out_specs=(P("expert", None, "hidden"), P("expert", None, "hidden"), P("expert", None)),
        check_vma=False,
    )
```

profile of v0, /device:TPU:33, one launch (start us, length us, event | category | flops | bytes accessed | tf_op | source)
XLA Modules:
  0.0 364.0 jit_solution(17710383384347243278)
XLA Ops:
  0.6 1.3 fusion.66
  1.9 0.1 copy.111
  2.1 0.2 broadcast_in_dim.12
  2.3 60.5 %all_to_all.101 = f32[4,2,196,128]{3,1,2,0:T(2,128)S(1)} all-to-all(f32[4,2,196,128]{3,1,2,0:T(2,128)S(1)} %broadcast_in_dim.12), channel_id=1, replica_groups=mesh['expert'=128,'hidden'=4] {'hidden'}, dimensions={0} | all-to-all | bytes 1605632 | tf_op jit(solution)/shard_map/all_to_all | solution.py:11
  62.8 0.4 reduce_sum.95
  63.2 0.3 fusion.98
  63.5 0.9 exponential_reduce_fusion
  64.4 1.2 fusion.99
  65.6 1.2 convolution_convert_fusion.2
  66.8 0.8 copy.114
  67.6 11.4 %all-to-all-start.1 = ((bf16[2,128,256]{2,0,1:T(2,128)(2,1)}), bf16[2,128,256]{2,0,1:T(2,128)(2,1)S(1)}, u32[]{:S(2)}, u32[]{:S(2)}) async-start(bf16[2,128,256]{2,0,1:T(2,128)(2,1)} %copy.114), calls=%async_computation.1 | async-start | bytes 262144 | tf_op jit(solution)/shard_map/all_to_all | solution.py:75
  79.0 0.2 convolution_convert_fusion.1
  79.3 0.8 copy.126
  80.0 12.7 %all-to-all-done.1 = bf16[2,128,256]{2,0,1:T(2,128)(2,1)S(1)} async-done(((bf16[2,128,256]{2,0,1:T(2,128)(2,1)}), bf16[2,128,256]{2,0,1:T(2,128)(2,1)S(1)}, u32[]{:S(2)}, u32[]{:S(2)}) %all-to-all-start.1) | async-done | bytes 131104 | tf_op jit(solution)/shard_map/all_to_all | solution.py:75
  92.7 9.6 %all-to-all-start.6 = ((bf16[2,128,256]{2,0,1:T(2,128)(2,1)}), bf16[2,128,256]{2,0,1:T(2,128)(2,1)S(1)}, u32[]{:S(2)}, u32[]{:S(2)}) async-start(bf16[2,128,256]{2,0,1:T(2,128)(2,1)} %copy.126), calls=%async_computation.6 | async-start | bytes 262144 | tf_op jit(solution)/shard_map/all_to_all | solution.py:105
  102.3 0.1 copy.115
  102.4 13.5 %all-to-all-done.6 = bf16[2,128,256]{2,0,1:T(2,128)(2,1)S(1)} async-done(((bf16[2,128,256]{2,0,1:T(2,128)(2,1)}), bf16[2,128,256]{2,0,1:T(2,128)(2,1)S(1)}, u32[]{:S(2)}, u32[]{:S(2)}) %all-to-all-start.6) | async-done | bytes 131104 | tf_op jit(solution)/shard_map/all_to_all | solution.py:105
  116.0 0.8 broadcast_in_dim.13
  116.8 6.2 %all-to-all-start.2 = ((bf16[4,256,1,256]{1,3,2,0:T(8,128)(2,1)}), bf16[4,256,1,256]{1,3,2,0:T(8,128)(2,1)S(1)}, u32[]{:S(2)}, u32[]{:S(2)}) async-start(bf16[4,256,1,256]{1,3,2,0:T(8,128)(2,1)} %broadcast_in_dim.13), calls=%async_computation.2 | async-start | bytes 1048576 | tf_op jit(solution)/shard_map/all_to_all | solution.py:11
  123.0 0.1 copy.127
  123.2 33.7 %all-to-all-done.2 = bf16[4,256,1,256]{1,3,2,0:T(8,128)(2,1)S(1)} async-done(((bf16[4,256,1,256]{1,3,2,0:T(8,128)(2,1)}), bf16[4,256,1,256]{1,3,2,0:T(8,128)(2,1)S(1)}, u32[]{:S(2)}, u32[]{:S(2)}) %all-to-all-start.2) | async-done | bytes 524320 | tf_op jit(solution)/shard_map/all_to_all | solution.py:11
  156.8 0.9 broadcast_in_dim.32
  157.7 4.2 %all-to-all-start.7 = ((bf16[4,256,1,256]{1,3,2,0:T(8,128)(2,1)}), bf16[4,256,1,256]{1,3,2,0:T(8,128)(2,1)S(1)}, u32[]{:S(2)}, u32[]{:S(2)}) async-start(bf16[4,256,1,256]{1,3,2,0:T(8,128)(2,1)} %broadcast_in_dim.32), calls=%async_computation.7 | async-start | bytes 1048576 | tf_op jit(solution)/shard_map/all_to_all | solution.py:11
  161.9 0.7 add.77
  162.6 1.7 fusion.21
  164.3 16.9 %all-to-all-done.7 = bf16[4,256,1,256]{1,3,2,0:T(8,128)(2,1)S(1)} async-done(((bf16[4,256,1,256]{1,3,2,0:T(8,128)(2,1)}), bf16[4,256,1,256]{1,3,2,0:T(8,128)(2,1)S(1)}, u32[]{:S(2)}, u32[]{:S(2)}) %all-to-all-start.7) | async-done | bytes 524320 | tf_op jit(solution)/shard_map/all_to_all | solution.py:11
  181.2 3.7 %fusion.24 = bf16[256,1024]{1,0:T(8,128)(2,1)S(1)} fusion(bf16[1,1024,1024]{2,1,0:T(8,128)(2,1)S(1)} %copy-done, bf16[256,1024]{0,1:T(8,128)(2,1)S(1)} %bitcast.139, bf16[1,1024,1024]{2,1,0:T(8,128)(2,1)} %param.11, f32[256,1,1024]{2,0,1:T(8,128)} %fusion.21), kind=kOutput, calls=%fused_computation.16 | convolution fusion | flops 1078984704 | bytes 6291456 | tf_op jit(solution)/shard_map/ref,ekf->rek/dot_general | solution.py:113
  184.8 0.9 copy.182
  185.7 10.1 %all-to-all-start.8 = ((bf16[4,256,1,256]{3,1,2,0:T(8,128)(2,1)}), bf16[4,256,1,256]{3,1,2,0:T(8,128)(2,1)S(1)}, u32[]{:S(2)}, u32[]{:S(2)}) async-start(bf16[4,256,1,256]{3,1,2,0:T(8,128)(2,1)} %bitcast.134), calls=%async_computation.8 | async-start | bytes 1048576 | tf_op jit(solution)/shard_map/all_to_all | solution.py:37
  195.8 2.7 fusion.27
  198.6 0.8 copy.183
  199.4 13.6 %all-to-all-done.8 = bf16[4,256,1,256]{3,1,2,0:T(8,128)(2,1)S(1)} async-done(((bf16[4,256,1,256]{3,1,2,0:T(8,128)(2,1)}), bf16[4,256,1,256]{3,1,2,0:T(8,128)(2,1)S(1)}, u32[]{:S(2)}, u32[]{:S(2)}) %all-to-all-start.8) | async-done | bytes 524320 | tf_op jit(solution)/shard_map/all_to_all | solution.py:37
  213.0 4.3 %all-to-all-start.3 = ((bf16[4,256,1,256]{3,1,2,0:T(8,128)(2,1)}), bf16[4,256,1,256]{3,1,2,0:T(8,128)(2,1)S(1)}, u32[]{:S(2)}, u32[]{:S(2)}) async-start(bf16[4,256,1,256]{3,1,2,0:T(8,128)(2,1)} %bitcast.138), calls=%async_computation.3 | async-start | bytes 1048576 | tf_op jit(solution)/shard_map/all_to_all | solution.py:37
  217.3 0.7 reduce_sum.103
  218.0 1.6 reshape.121
  219.7 16.2 %all-to-all-done.3 = bf16[4,256,1,256]{3,1,2,0:T(8,128)(2,1)S(1)} async-done(((bf16[4,256,1,256]{3,1,2,0:T(8,128)(2,1)}), bf16[4,256,1,256]{3,1,2,0:T(8,128)(2,1)S(1)}, u32[]{:S(2)}, u32[]{:S(2)}) %all-to-all-start.3) | async-done | bytes 524320 | tf_op jit(solution)/shard_map/all_to_all | solution.py:37
  235.8 23.5 %all-to-all-start.9 = ((bf16[128,2,1,256]{3,1,2,0:T(2,128)(2,1)}), bf16[128,2,1,256]{3,1,2,0:T(2,128)(2,1)}, u32[]{:S(2)}, u32[]{:S(2)}) async-start(bf16[128,2,1,256]{3,1,2,0:T(2,128)(2,1)} %bitcast.37), calls=%async_computation.9 | async-start | bytes 262144 | tf_op jit(solution)/shard_map/all_to_all | solution.py:115
  259.3 1.2 convert_element_type.119
  260.7 0.1 reduce_sum.99
  260.8 0.7 fusion.61
  261.5 0.8 copy.119
  262.3 11.3 %all-to-all-done.9 = bf16[128,2,1,256]{3,1,2,0:T(2,128)(2,1)} async-done(((bf16[128,2,1,256]{3,1,2,0:T(2,128)(2,1)}), bf16[128,2,1,256]{3,1,2,0:T(2,128)(2,1)}, u32[]{:S(2)}, u32[]{:S(2)}) %all-to-all-start.9) | async-done | bytes 131104 | tf_op jit(solution)/shard_map/all_to_all | solution.py:115
  273.6 8.7 %all-to-all-start.4 = ((bf16[128,2,1,256]{3,1,2,0:T(2,128)(2,1)}), bf16[128,2,1,256]{3,1,2,0:T(2,128)(2,1)S(1)}, u32[]{:S(2)}, u32[]{:S(2)}) async-start(bf16[128,2,1,256]{3,1,2,0:T(2,128)(2,1)} %copy.119), calls=%async_computation.4 | async-start | bytes 262144 | tf_op jit(solution)/shard_map/all_to_all | solution.py:88
  282.2 1.2 fusion.43
  283.4 0.1 copy.133
  283.5 12.4 %all-to-all-done.4 = bf16[128,2,1,256]{3,1,2,0:T(2,128)(2,1)S(1)} async-done(((bf16[128,2,1,256]{3,1,2,0:T(2,128)(2,1)}), bf16[128,2,1,256]{3,1,2,0:T(2,128)(2,1)S(1)}, u32[]{:S(2)}, u32[]{:S(2)}) %all-to-all-start.4) | async-done | bytes 131104 | tf_op jit(solution)/shard_map/all_to_all | solution.py:88
  295.9 0.9 broadcast_in_dim.33
  296.9 8.9 %all-to-all-start.10 = ((bf16[4,2,196,128]{3,1,2,0:T(2,128)(2,1)}), bf16[4,2,196,128]{3,1,2,0:T(2,128)(2,1)S(1)}, u32[]{:S(2)}, u32[]{:S(2)}) async-start(bf16[4,2,196,128]{3,1,2,0:T(2,128)(2,1)} %broadcast_in_dim.33), calls=%async_computation.10 | async-start | bytes 802816 | tf_op jit(solution)/shard_map/all_to_all | solution.py:11
  305.8 0.2 fusion.42
  306.1 28.3 %all-to-all-done.10 = bf16[4,2,196,128]{3,1,2,0:T(2,128)(2,1)S(1)} async-done(((bf16[4,2,196,128]{3,1,2,0:T(2,128)(2,1)}), bf16[4,2,196,128]{3,1,2,0:T(2,128)(2,1)S(1)}, u32[]{:S(2)}, u32[]{:S(2)}) %all-to-all-start.10) | async-done | bytes 401440 | tf_op jit(solution)/shard_map/all_to_all | solution.py:11
  334.3 0.9 broadcast_in_dim.14
  335.3 4.2 %all-to-all-start.5 = ((bf16[4,2,196,128]{3,1,2,0:T(2,128)(2,1)}), bf16[4,2,196,128]{3,1,2,0:T(2,128)(2,1)S(1)}, u32[]{:S(2)}, u32[]{:S(2)}) async-start(bf16[4,2,196,128]{3,1,2,0:T(2,128)(2,1)} %broadcast_in_dim.14), calls=%async_computation.5 | async-start | bytes 802816 | tf_op jit(solution)/shard_map/all_to_all | solution.py:11
  339.4 0.7 multiply_multiply_fusion.1
  340.1 0.7 copy.138
  340.8 0.2 convolution_convert_fusion
  341.0 0.8 copy.136
  341.8 0.4 convert_reduce_fusion.1
  342.2 1.2 multiply_reduce_fusion
  343.4 14.1 %all-to-all-done.5 = bf16[4,2,196,128]{3,1,2,0:T(2,128)(2,1)S(1)} async-done(((bf16[4,2,196,128]{3,1,2,0:T(2,128)(2,1)}), bf16[4,2,196,128]{3,1,2,0:T(2,128)(2,1)S(1)}, u32[]{:S(2)}, u32[]{:S(2)}) %all-to-all-start.5) | async-done | bytes 401440 | tf_op jit(solution)/shard_map/all_to_all | solution.py:11
  357.5 0.4 convert_reduce_fusion.2
  357.9 3.9 %fusion.41 = bf16[2,196,128]{2,0,1:T(2,128)(2,1)S(1)} fusion(f32[2,196,128]{2,0,1:T(2,128)} %get-tuple-element.27, f32[2,196,128]{2,0,1:T(2,128)S(1)} %convert_reduce_fusion.2, f32[2,196,128]{2,0,1:T(2,128)} %get-tuple-element.33, f32[2,196,128]{2,0,1:T(2,128)S(1)} %convert_reduce_fusion.1, f32[2,128]{1,0:T(2,128)S(1)} %multiply_reduce_fusion, ...), kind=kOutput, calls=%fused_computation.31 | output fusion | flops 401927 | bytes 905760 | tf_op jit(solution)/shard_map/sub | solution.py:129
  361.8 0.2 fusion.81
  362.0 1.1 fusion.36
  363.1 0.8 copy.137
  (15 shorter events, 0.3 us)
Async XLA Ops:
  0.6 161.9 %copy-start = (bf16[1,1024,1024]{2,1,0:T(8,128)(2,1)S(1)}, bf16[1,1024,1024]{2,1,0:T(8,128)(2,1)}, u32[]{:S(2)}) copy-start(bf16[1,1024,1024]{2,1,0:T(8,128)(2,1)} %param.9) | copy-start | bytes 6291460
  63.2 15.8 %copy-start.2 = (bf16[2,196,256]{2,0,1:T(2,128)(2,1)S(1)}, bf16[2,196,256]{2,0,1:T(2,128)(2,1)}, u32[]{:S(2)}) copy-start(bf16[2,196,256]{2,0,1:T(2,128)(2,1)} %param.13) | copy-start | bytes 602116
  67.6 25.1 %all-to-all-start.1 = ((bf16[2,128,256]{2,0,1:T(2,128)(2,1)}), bf16[2,128,256]{2,0,1:T(2,128)(2,1)S(1)}, u32[]{:S(2)}, u32[]{:S(2)}) async-start(bf16[2,128,256]{2,0,1:T(2,128)(2,1)} %copy.114), calls=%async_computation.1 | async-start | bytes 262144 | tf_op jit(solution)/shard_map/all_to_all | solution.py:75
  92.7 23.3 %all-to-all-start.6 = ((bf16[2,128,256]{2,0,1:T(2,128)(2,1)}), bf16[2,128,256]{2,0,1:T(2,128)(2,1)S(1)}, u32[]{:S(2)}, u32[]{:S(2)}) async-start(bf16[2,128,256]{2,0,1:T(2,128)(2,1)} %copy.126), calls=%async_computation.6 | async-start | bytes 262144 | tf_op jit(solution)/shard_map/all_to_all | solution.py:105
  116.8 40.0 %all-to-all-start.2 = ((bf16[4,256,1,256]{1,3,2,0:T(8,128)(2,1)}), bf16[4,256,1,256]{1,3,2,0:T(8,128)(2,1)S(1)}, u32[]{:S(2)}, u32[]{:S(2)}) async-start(bf16[4,256,1,256]{1,3,2,0:T(8,128)(2,1)} %broadcast_in_dim.13), calls=%async_computation.2 | async-start | bytes 1048576 | tf_op jit(solution)/shard_map/all_to_all | solution.py:11
  157.7 23.5 %all-to-all-start.7 = ((bf16[4,256,1,256]{1,3,2,0:T(8,128)(2,1)}), bf16[4,256,1,256]{1,3,2,0:T(8,128)(2,1)S(1)}, u32[]{:S(2)}, u32[]{:S(2)}) async-start(bf16[4,256,1,256]{1,3,2,0:T(8,128)(2,1)} %broadcast_in_dim.32), calls=%async_computation.7 | async-start | bytes 1048576 | tf_op jit(solution)/shard_map/all_to_all | solution.py:11
  185.7 27.3 %all-to-all-start.8 = ((bf16[4,256,1,256]{3,1,2,0:T(8,128)(2,1)}), bf16[4,256,1,256]{3,1,2,0:T(8,128)(2,1)S(1)}, u32[]{:S(2)}, u32[]{:S(2)}) async-start(bf16[4,256,1,256]{3,1,2,0:T(8,128)(2,1)} %bitcast.134), calls=%async_computation.8 | async-start | bytes 1048576 | tf_op jit(solution)/shard_map/all_to_all | solution.py:37
  213.0 22.8 %all-to-all-start.3 = ((bf16[4,256,1,256]{3,1,2,0:T(8,128)(2,1)}), bf16[4,256,1,256]{3,1,2,0:T(8,128)(2,1)S(1)}, u32[]{:S(2)}, u32[]{:S(2)}) async-start(bf16[4,256,1,256]{3,1,2,0:T(8,128)(2,1)} %bitcast.138), calls=%async_computation.3 | async-start | bytes 1048576 | tf_op jit(solution)/shard_map/all_to_all | solution.py:37
  235.8 37.7 %all-to-all-start.9 = ((bf16[128,2,1,256]{3,1,2,0:T(2,128)(2,1)}), bf16[128,2,1,256]{3,1,2,0:T(2,128)(2,1)}, u32[]{:S(2)}, u32[]{:S(2)}) async-start(bf16[128,2,1,256]{3,1,2,0:T(2,128)(2,1)} %bitcast.37), calls=%async_computation.9 | async-start | bytes 262144 | tf_op jit(solution)/shard_map/all_to_all | solution.py:115
  260.6 45.1 %copy-start.3 = (bf16[2,196,256]{2,0,1:T(2,128)(2,1)S(1)}, bf16[2,196,256]{2,0,1:T(2,128)(2,1)}, u32[]{:S(2)}) copy-start(bf16[2,196,256]{2,0,1:T(2,128)(2,1)} %param.13) | copy-start | bytes 602116
  273.6 22.4 %all-to-all-start.4 = ((bf16[128,2,1,256]{3,1,2,0:T(2,128)(2,1)}), bf16[128,2,1,256]{3,1,2,0:T(2,128)(2,1)S(1)}, u32[]{:S(2)}, u32[]{:S(2)}) async-start(bf16[128,2,1,256]{3,1,2,0:T(2,128)(2,1)} %copy.119), calls=%async_computation.4 | async-start | bytes 262144 | tf_op jit(solution)/shard_map/all_to_all | solution.py:88
  296.9 37.5 %all-to-all-start.10 = ((bf16[4,2,196,128]{3,1,2,0:T(2,128)(2,1)}), bf16[4,2,196,128]{3,1,2,0:T(2,128)(2,1)S(1)}, u32[]{:S(2)}, u32[]{:S(2)}) async-start(bf16[4,2,196,128]{3,1,2,0:T(2,128)(2,1)} %broadcast_in_dim.33), calls=%async_computation.10 | async-start | bytes 802816 | tf_op jit(solution)/shard_map/all_to_all | solution.py:11
  335.3 22.2 %all-to-all-start.5 = ((bf16[4,2,196,128]{3,1,2,0:T(2,128)(2,1)}), bf16[4,2,196,128]{3,1,2,0:T(2,128)(2,1)S(1)}, u32[]{:S(2)}, u32[]{:S(2)}) async-start(bf16[4,2,196,128]{3,1,2,0:T(2,128)(2,1)} %broadcast_in_dim.14), calls=%async_computation.5 | async-start | bytes 802816 | tf_op jit(solution)/shard_map/all_to_all | solution.py:11
  340.1 17.8 %copy-start.4 = (f32[2,196]{0,1:T(8,128)S(1)}, f32[2,196]{0,1:T(8,128)}, u32[]{:S(2)}) copy-start(f32[2,196]{0,1:T(8,128)} %get-tuple-element.31) | copy-start | bytes 4708
  341.8 20.0 %copy-start.1 = (bf16[256,128]{1,0:T(8,128)(2,1)S(1)}, bf16[256,128]{1,0:T(8,128)(2,1)}, u32[]{:S(2)}) copy-start(bf16[256,128]{1,0:T(8,128)(2,1)} %param.8) | copy-start | bytes 196612
where the time goes:
time: 365 us; the launch traced here: 364 us
  waiting for transfers between devices  173 us (47%)
  starting transfers between devices  91 us (25%)
  blocking collectives  60.5 us (17%)
  matrix products  13.7 us (4%)
  other arithmetic  12.8 us (4%)
  local copies, waits for them, and re-layouts  12.5 us (3%)
    all_to_all x4, waiting for transfers between devices, sent_to_all(): return lax.all_to_all(copies, axis, split_axis=0, concat_axis=0, tiled=True)  93 us
    all_to_all x1, blocking collectives, sent_to_all(): return lax.all_to_all(copies, axis, split_axis=0, concat_axis=0, tiled=True)  60.5 us
    all_to_all x2, waiting for transfers between devices, sent_and_summed(): tiles = lax.all_to_all(split_up(x, dim, peers), axis, 0, 0, tiled=True)  29.8 us
    all_to_all x1, starting transfers between devices, per_device(): lax.all_to_all(slot_grad.reshape(groups, images_dev, local_experts, quart...  23.5 us
    all_to_all x4, starting transfers between devices, sent_to_all(): return lax.all_to_all(copies, axis, split_axis=0, concat_axis=0, tiled=True)  23.5 us
    all_to_all x2, starting transfers between devices, sent_and_summed(): tiles = lax.all_to_all(split_up(x, dim, peers), axis, 0, 0, tiled=True)  14.4 us
    all_to_all x1, waiting for transfers between devices, per_device(): lax.all_to_all(out_grad, 'expert', split_axis=1, concat_axis=0, tiled=True)  13.5 us
    all_to_all x1, waiting for transfers between devices, per_device(): lax.all_to_all(slot_in, 'expert', split_axis=1, concat_axis=0, tiled=True)  12.7 us
  transfers between devices with their start and end apart: 10, of which 10 were waited for; matrix products, arithmetic and copies ran while one was open for 5% of the time, Pallas kernels for 0%

commit v1 on v0

v1 whole, which is shorter than its diff:
```python
import jax
import jax.numpy as jnp
from jax import lax
from jax.experimental import pallas as pl
from jax.experimental.pallas import tpu as pltpu
from jax.sharding import PartitionSpec as P

loss_weight = 0.1
MESH = pl.DeviceIdType.MESH
F32, BF16 = jnp.float32, jnp.bfloat16

IMG, TOK, TP, HALF, QF, SLOTS = 2, 196, 208, 104, 256, 128
NJ, NZ, NZL = 16, 16, 8


def gelu_parts(value):
    factor = 0.7978845608028654
    inner = factor * (value + 0.044715 * value * value * value)
    slope_tanh = jnp.tanh(inner)
    result = 0.5 * value * (1.0 + slope_tanh)
    slope = 0.5 * (1.0 + slope_tanh) + 0.5 * value * (1.0 - slope_tanh * slope_tanh) * factor * (
        1.0 + 3.0 * 0.044715 * value * value
    )
    return result, slope


def dot(a, b, ca, cb):
    return lax.dot_general(a, b, (((ca,), (cb,)), ((), ())), preferred_element_type=F32)


def kernel(
    tok, sp, w1_hbm, bi, w2_hbm, bo, cot,
    mixed, tgrad, zloss,
    w1, w2, wsem,
    lp, la, lzs, lzr, lf,
    disp, comb, tcomb, dlow, clow,
    s, r1, fa, r2, x,
    act, slope, px_s, px_r, cs, y, fb, q, v,
    gp, ga, gzs, gzr, gf,
    a1s, a1r, a2s, a2r, a3s, a3r, b1s, b1r, b2s, b2r, fws, fwr,
    pxs, pxr, c1s, c1r, c2s, c2r, d1s, d1r, d2s, d2r, d3s, d3r,
):
    e, h = lax.axis_index("expert"), lax.axis_index("hidden")
    j, zl, zh, c = e // NZL, e % NZL, h // 2, h % 2
    z = zh * NZL + zl
    core_peer = (e, zh * 2 + 1 - c)
    z8_peer = (e, (1 - zh) * 2 + c)

    def z_at(d):
        return (z + d) % NZ

    def z_dev(zz):
        return (j * NZL + zz % NZL, (zz // NZL) * 2 + c)

    def j_at(d):
        yy, xx = (j // 4 + d // 4) % 4, (j % 4 + d % 4) % 4
        return yy * 4 + xx

    def j_from(d):
        yy, xx = (j // 4 + 4 - d // 4) % 4, (j % 4 + 4 - d % 4) % 4
        return yy * 4 + xx

    def j_dev(jj):
        return (jj * NZL + zl, h)

    def rc(src, dst, ss, rs, dev):
        return pltpu.make_async_remote_copy(
            src_ref=src, dst_ref=dst, send_sem=ss, recv_sem=rs, device_id=dev, device_id_type=MESH
        )

    def each(n, body, start=1):
        lax.fori_loop(start, n, lambda k, carry: (body(k), carry)[1], 0)

    barrier = pltpu.get_barrier_semaphore()
    pl.semaphore_signal(barrier, inc=1, device_id=core_peer, device_id_type=MESH)
    each(NZ, lambda d: pl.semaphore_signal(barrier, inc=1, device_id=z_dev(z_at(d)), device_id_type=MESH))
    each(NJ, lambda d: pl.semaphore_signal(barrier, inc=1, device_id=j_dev(j_at(d)), device_id_type=MESH))
    w1_copy = pltpu.make_async_copy(w1_hbm, w1, wsem.at[0])
    w2_copy = pltpu.make_async_copy(w2_hbm, w2, wsem.at[1])
    w1_copy.start()
    w2_copy.start()

    mine, theirs = pl.ds(pl.multiple_of(c * HALF, 8), HALF), pl.ds(pl.multiple_of((1 - c) * HALF, 8), HALF)

    for i in range(IMG):
        lp[i] = dot(tok[i], sp[...], 1, 0)
    pl.semaphore_wait(barrier, 1 + (NZ - 1) + (NJ - 1))

    def a1(i):
        return rc(lp.at[i, theirs], la.at[i], a1s.at[i], a1r.at[i], core_peer)

    def a2(i):
        return rc(lzs.at[i], lzr.at[i], a2s.at[i], a2r.at[i], z8_peer)

    def a3(i, rows):
        return rc(lf.at[i, rows], lf.at[i, rows], a3s.at[i], a3r.at[i], core_peer)

    def b1(i, d, src, dst):
        return rc(s.at[i, :, src], r1.at[i, :, dst], b1s.at[i, d], b1r.at[i, d], j_dev(j_at(d)))

    def b2(i, d, src, half, low):
        return rc(r2.at[i, src], x.at[i, half * 2 + c, low], b2s.at[i, d], b2r.at[i, d], z_dev(z_at(d)))

    def fwd(i, d, quarter, low):
        return rc(x.at[i, quarter, low], x.at[i, quarter, low], fws.at[i, d], fwr.at[i, d], core_peer)

    def px(i, t):
        return rc(px_s.at[i, t], px_r.at[i, t], pxs.at[i, t], pxr.at[i, t], core_peer)

    def c1(i, t, d, sh, sl, dh, dl):
        return rc(cs.at[i, t, sh, sl], y.at[i, t, dh, dl], c1s.at[i, t, d], c1r.at[i, t, d], z_dev(z_at(d)))

    def c2(i, t, d, src, dst):
        return rc(q.at[i, t, src], v.at[i, t, dst], c2s.at[i, t, d], c2r.at[i, t, d], j_dev(j_at(d)))

    def d1(i):
        return rc(gp.at[i, theirs], ga.at[i], d1s.at[i], d1r.at[i], core_peer)

    def d2(i):
        return rc(gzs.at[i], gzr.at[i], d2s.at[i], d2r.at[i], z8_peer)

    def d3(i, rows):
        return rc(gf.at[i, rows], gf.at[i, rows], d3s.at[i], d3r.at[i], core_peer)

    def logits_across(i):
        a1(i).wait_recv()
        lzs[i] = lp[i, mine] + la[i]
        a2(i).start()

    def logits_whole(i):
        a2(i).wait_recv()
        lf[i, mine] = lzs[i] + lzr[i]
        a3(i, mine).start()

    def softmaxes(i):
        a3(i, theirs).wait_recv()
        logits = lf[i]
        row = lax.broadcasted_iota(jnp.int32, (TP, SLOTS), 0)
        masked = jnp.where(row < TOK, logits, -1e30)
        top = jnp.max(masked, axis=0, keepdims=True)
        up = jnp.exp(masked - top)
        dispatch = up / jnp.sum(up, axis=0, keepdims=True)
        disp[i] = dispatch
        dispatch_low = dispatch.astype(BF16)
        dlow[i] = dispatch_low
        s[i, 0] = dot(dispatch_low, tok[i], 0, 0).reshape(NJ, 8, QF).astype(BF16)
        top = jnp.max(logits, axis=1, keepdims=True)
        up = jnp.exp(logits - top)
        below = jnp.sum(up, axis=1, keepdims=True)
        combine = up / below
        comb[i] = combine
        combine_low = combine.astype(BF16)
        clow[i] = combine_low
        s[i, 1] = dot(combine_low, cot[i], 0, 0).reshape(NJ, 8, QF).astype(BF16)
        each(NJ, lambda d: b1(i, d, j_at(d), j).start())
        r1[i, :, j] = s[i, :, j]
        total = top + jnp.log(below)
        tcomb[i] = (2.0 * loss_weight) * total * combine
        wide = jnp.broadcast_to(loss_weight * total * total, (TP, SLOTS))
        zloss[i] = jnp.transpose(wide)[0:8, :]

    def to_experts(i):
        each(NJ, lambda d: b1(i, d, j_at(d), j_from(d)).wait_recv())
        for t in range(2):
            rows = r1[i, t].astype(F32).reshape(SLOTS, QF)
            for lanes in range(2):
                fa[t, lanes] = rows[:, lanes * 128 : (lanes + 1) * 128]
        for low in range(NZL):
            for t in range(2):
                rows = [fa[t, lanes, pl.ds(low, NJ, stride=8), :] for lanes in range(2)]
                r2[i, low, t] = jnp.concatenate(rows, axis=1).astype(BF16)
        each(NZ, lambda d: b2(i, d, z_at(d) % NZL, zh, zl).start())
        x[i, h, zl] = r2[i, zl]

    def near_first(k):
        return lax.select(k % 2 == 1, (k + 1) // 2, NZ - k // 2)

    def arrive(i):
        fwd(i, 0, h, zl).start()

        def one(k):
            d = near_first(k)
            src = z_at(NZ - d)
            b2(i, d, z_at(d) % NZL, src // NZL, src % NZL).wait_recv()
            fwd(i, d, (src // NZL) * 2 + c, src % NZL).start()

        each(NZ, one)

        def other(d):
            src = z_at(NZ - d)
            fwd(i, d, (src // NZL) * 2 + 1 - c, src % NZL).wait_recv()

        each(NZ, other, 0)

    def rows_of(i, t):
        return jnp.concatenate([x[i, k, :, t].reshape(SLOTS, QF) for k in range(4)], axis=1)

    def quarter(k, core):
        return pl.ds(pl.multiple_of((k * 2 + core) * QF, QF), QF)

    FB = 256

    def expert(i):
        arrived = rows_of(i, 0)
        for f in range(0, 1024, FB):
            part = dot(arrived, w1[:, f : f + FB], 1, 0) + bi[:, f : f + FB].astype(F32)
            activated, slope_part = gelu_parts(part)
            act[0, :, f : f + FB] = activated.astype(BF16)
            slope[:, f : f + FB] = slope_part
        send_results(i, 0, lambda cols: dot(act[0], w2[:, cols], 1, 0))
        arrived = rows_of(i, 1)
        for f in range(0, 1024, FB):
            part = dot(arrived, w2[f : f + FB, :], 1, 1) * slope[:, f : f + FB]
            act[1, :, f : f + FB] = part.astype(BF16)
        send_results(i, 1, lambda cols: dot(act[1], w1[cols, :], 1, 1))

    def send_results(i, t, product):
        for k in range(2):
            px_s[i, t, k] = product(quarter(k, 1 - c)).astype(BF16)
        px(i, t).start()
        own = [product(quarter(k, c)) for k in range(2)]
        px(i, t).wait_recv()
        for k in range(2):
            total = own[k] + px_r[i, t, k].astype(F32)
            if t == 0:
                total = total + jnp.where(zh == k, 1.0, 0.0) * bo[...].astype(F32)
            cs[i, t, k] = total.reshape(NZL, NJ, QF).astype(BF16)
        each(NZ, lambda d: c1(i, t, d, z_at(d) // NZL, z_at(d) % NZL, zh, zl).start())
        y[i, t, zh, zl] = cs[i, t, zh, zl]

    def to_images(i, t):
        def arrived(d):
            src = z_at(NZ - d)
            c1(i, t, d, z_at(d) // NZL, z_at(d) % NZL, src // NZL, src % NZL).wait_recv()

        each(NZ, arrived)
        for low in range(NZL):
            rows = y[i, t, 0, low].astype(F32) + y[i, t, 1, low].astype(F32)
            for lanes in range(2):
                fb[t, lanes, pl.ds(low, NJ, stride=8), :] = rows[:, lanes * 128 : (lanes + 1) * 128]
        rows = jnp.concatenate([fb[t, lanes] for lanes in range(2)], axis=1)
        q[i, t] = rows.reshape(NJ, 8, QF).astype(BF16)
        each(NJ, lambda d: c2(i, t, d, j_at(d), j).start())
        v[i, t, j] = q[i, t, j]

    def back(i, t):
        each(NJ, lambda d: c2(i, t, d, j_at(d), j_from(d)).wait_recv())
        return v[i, t].astype(F32).reshape(SLOTS, QF).astype(BF16)

    def gradients(i):
        slot_out = back(i, 0)
        mixed[i] = dot(clow[i], slot_out, 1, 0).astype(BF16)
        combine_grad = dot(cot[i], slot_out, 1, 1)
        combine = comb[i]
        part = combine * (combine_grad - jnp.sum(combine * combine_grad, axis=1, keepdims=True))
        in_grad = back(i, 1)
        dispatch_grad = dot(tok[i], in_grad, 1, 1)
        dispatch = disp[i]
        part += dispatch * (dispatch_grad - jnp.sum(dispatch * dispatch_grad, axis=0, keepdims=True))
        gp[i] = part
        d1(i).start()

    def gradients_across(i):
        d1(i).wait_recv()
        half = gp[i, mine] + ga[i]
        gzs[i] = half.astype(BF16)
        d2(i).start()
        ga[i] = half

    def gradients_whole(i):
        d2(i).wait_recv()
        half = ga[i] + gzr[i].astype(F32) + tcomb[i, mine]
        gf[i, mine] = half.astype(BF16).astype(F32)
        d3(i, mine).start()

    def finish(i):
        in_grad = v[i, 1].astype(F32).reshape(SLOTS, QF).astype(BF16)
        result = dot(dlow[i], in_grad, 1, 0)
        d3(i, theirs).wait_recv()
        tgrad[i] = (result + dot(gf[i].astype(BF16), sp[...], 1, 1)).astype(BF16)

    logits_send = [a1(i) for i in range(IMG)]
    for copy in logits_send:
        copy.start()
    logits_across(0)
    logits_across(1)
    logits_whole(0)
    softmaxes(0)
    logits_whole(1)
    softmaxes(1)
    to_experts(0)
    to_experts(1)
    arrive(0)
    w1_copy.wait()
    w2_copy.wait()
    expert(0)
    arrive(1)
    expert(1)
    to_images(0, 0)
    to_images(0, 1)
    gradients(0)
    gradients_across(0)
    to_images(1, 0)
    to_images(1, 1)
    gradients_whole(0)
    gradients(1)
    finish(0)
    gradients_across(1)
    gradients_whole(1)
    finish(1)

    for i in range(IMG):
        for copy in (a1(i), a2(i), a3(i, mine), d1(i), d2(i), d3(i, mine)):
            copy.wait_send()
        each(NJ, lambda d: b1(i, d, j_at(d), j).wait_send())
        each(NZ, lambda d: b2(i, d, z_at(d) % NZL, zh, zl).wait_send())
        each(NZ, lambda d: fwd(i, d, (z_at(NZ - d) // NZL) * 2 + c, z_at(NZ - d) % NZL).wait_send(), 0)
        for t in range(2):
            px(i, t).wait_send()
            each(NZ, lambda d: c1(i, t, d, z_at(d) // NZL, z_at(d) % NZL, zh, zl).wait_send())
            each(NJ, lambda d: c2(i, t, d, j_at(d), j).wait_send())


def per_device(tokens, slot_params, weight_in, bias_in, weight_out, bias_out, cotangent):
    vmem = pl.BlockSpec(memory_space=pltpu.VMEM)
    hbm = pl.BlockSpec(memory_space=pl.ANY)
    dma = pltpu.SemaphoreType.DMA
    pad = ((0, 0), (0, TP - TOK), (0, 0))
    scratch = [
        ((1024, 1024), BF16),
        ((1024, 1024), BF16),
        dma((2,)),
        ((IMG, TP, SLOTS), F32),
        ((IMG, HALF, SLOTS), F32),
        ((IMG, HALF, SLOTS), F32),
        ((IMG, HALF, SLOTS), F32),
        ((IMG, TP, SLOTS), F32),
        ((IMG, TP, SLOTS), F32),
        ((IMG, TP, SLOTS), F32),
        ((IMG, TP, SLOTS), F32),
        ((IMG, TP, SLOTS), BF16),
        ((IMG, TP, SLOTS), BF16),
        ((IMG, 2, NJ, 8, QF), BF16),
        ((IMG, 2, NJ, 8, QF), BF16),
        ((2, 2, SLOTS, 128), F32),
        ((IMG, NZL, 2, NJ, QF), BF16),
        ((IMG, 4, NZL, 2, NJ, QF), BF16),
        ((2, SLOTS, 1024), BF16),
        ((SLOTS, 1024), F32),
        ((IMG, 2, 2, SLOTS, QF), BF16),
        ((IMG, 2, 2, SLOTS, QF), BF16),
        ((IMG, 2, 2, NZL, NJ, QF), BF16),
        ((IMG, 2, 2, NZL, NJ, QF), BF16),
        ((2, 2, SLOTS, 128), F32),
        ((IMG, 2, NJ, 8, QF), BF16),
        ((IMG, 2, NJ, 8, QF), BF16),
        ((IMG, TP, SLOTS), F32),
        ((IMG, HALF, SLOTS), F32),
        ((IMG, HALF, SLOTS), BF16),
        ((IMG, HALF, SLOTS), BF16),
        ((IMG, TP, SLOTS), F32),
    ]
    scratch = [pltpu.VMEM(*a) if isinstance(a, tuple) else a for a in scratch]
    scratch += [dma((IMG,))] * 6 + [dma((IMG, NJ))] * 2 + [dma((IMG, NZ))] * 4 + [dma((IMG, 2))] * 2
    scratch += [dma((IMG, 2, NZ))] * 2 + [dma((IMG, 2, NJ))] * 2 + [dma((IMG,))] * 6
    mixed, token_grad, zloss = pl.pallas_call(
        kernel,
        out_shape=(
            jax.ShapeDtypeStruct((IMG, TP, QF), BF16),
            jax.ShapeDtypeStruct((IMG, TP, QF), BF16),
            jax.ShapeDtypeStruct((IMG, 8, TP), F32),
        ),
        in_specs=[vmem, vmem, hbm, vmem, hbm, vmem, vmem],
        out_specs=(vmem, vmem, vmem),
        scratch_shapes=scratch,
        compiler_params=pltpu.CompilerParams(
            collective_id=1, has_side_effects=True, vmem_limit_bytes=56 * 2**20
        ),
        name="layer",
    )(
        jnp.pad(tokens, pad),
        slot_params,
        weight_in.reshape(1024, 1024),
        bias_in,
        weight_out.reshape(1024, 1024),
        bias_out,
        jnp.pad(cotangent, pad),
    )
    return mixed[:, :TOK], token_grad[:, :TOK], zloss[:, 0, :TOK]


def solution(mesh):
    return jax.shard_map(
        per_device,
        mesh=mesh,
        in_specs=(
            P("expert", None, "hidden"),
            P("hidden", None),
            P("expert", None, "hidden"),
            P("expert", "hidden"),
            P("expert", "hidden", None),
            P("expert", "hidden"),
            P("expert", None, "hidden"),
        ),
        out_specs=(P("expert", None, "hidden"), P("expert", None, "hidden"), P("expert", None)),
        check_vma=False,
    )
```

time: 365 us -> 116 us (0.32)
  the two profiles are of different devices: /device:TPU:33 before, /device:TPU:1 now
where the time goes in v1:
time: 116 us; the launch traced here: 115 us
  Pallas kernels  107 us (92%)
  local copies, waits for them, and re-layouts  8.16 us (7%)
    pallas_call x1, Pallas kernels, per_device(): pl.pallas_call(kernel, out_shape=(jax.ShapeDtypeStruct((IMG, TP, QF), BF1...  107 us
    unnamed x5, local copies, waits for them, and re-layouts  4.15 us
    slice x3, local copies, waits for them, and re-layouts, per_device(): return (mixed[:, :TOK], token_grad[:, :TOK], zloss[:, 0, :TOK])  2.61 us

profile of v1, /device:TPU:1, one launch (start us, length us, event | category | flops | bytes accessed | tf_op | source)
XLA Modules:
  0.0 115.5 jit_solution(5751794811864152710)
XLA Ops:
  0.6 1.0 copy.10
  1.6 0.7 pad.7.tok
  2.3 0.9 copy.11
  3.2 0.7 pad.8.cot
  3.9 106.7 %layer.1 = (bf16[2,208,256]{2,1,0:T(8,128)(2,1)}, bf16[2,208,256]{2,1,0:T(8,128)(2,1)}, f32[2,8,208]{2,1,0:T(8,128)}) custom-call(bf16[2,208,256]{2,1,0:T(8,128)(2,1)} %pad.7.tok, bf16[256,128]{1,0:T(8,128)(2,1)} %sp.1, bf16[1024,1024]{1,0:T(8,128)(2,1)} %bitcast.5, bf16[1,1024]{1,0:T(2,128)(2,1)} %bi.1, bf16[1024,1024]{1,0:T(8,128)(2,1)} %bitcast.6, ...), custom_call_target="tpu_custom_call" | custom-call | tf_op jit(solution)/shard_map/layer/pallas_call | solution.py:366
  110.6 0.9 slice.9
  111.6 0.8 copy.12
  112.4 0.7 slice.11
  113.1 0.6 copy.16
  113.7 0.9 slice.10
  114.7 0.8 copy.13

commit v2 on v1

v2 whole, which is shorter than its diff:
```python
import jax
import jax.numpy as jnp
from jax import lax
from jax.experimental import pallas as pl
from jax.experimental.pallas import tpu as pltpu
from jax.sharding import PartitionSpec as P

loss_weight = 0.1
MESH = pl.DeviceIdType.MESH
F32, BF16 = jnp.float32, jnp.bfloat16

IMG, TOK, TP, HALF, QF, SLOTS = 2, 196, 208, 104, 256, 128
NJ, NZ, NZL = 16, 16, 8


def gelu_parts(value):
    factor = 0.7978845608028654
    inner = factor * (value + 0.044715 * value * value * value)
    slope_tanh = jnp.tanh(inner)
    result = 0.5 * value * (1.0 + slope_tanh)
    slope = 0.5 * (1.0 + slope_tanh) + 0.5 * value * (1.0 - slope_tanh * slope_tanh) * factor * (
        1.0 + 3.0 * 0.044715 * value * value
    )
    return result, slope


def dot(a, b, ca, cb):
    return lax.dot_general(a, b, (((ca,), (cb,)), ((), ())), preferred_element_type=F32)


def kernel(
    tok_in, sp, w1_hbm, bi, w2_hbm, bo, cot_in,
    mixed, tgrad, zloss,
    w1, w2, wsem, tok, cot,
    lp, la, lzs, lzr, lf,
    disp, comb, tcomb, dlow, clow,
    s, r1, fa, r2, x,
    act, slope, px_s, px_r, cs, y, fb, q, v,
    gp, ga, gzs, gzr, gf,
    a1s, a1r, a2s, a2r, a3s, a3r, b1s, b1r, b2s, b2r, fws, fwr,
    pxs, pxr, c1s, c1r, c2s, c2r, d1s, d1r, d2s, d2r, d3s, d3r,
):
    div, rem = lax.div, lax.rem
    e, h = lax.axis_index("expert"), lax.axis_index("hidden")
    j, zl, zh, c = div(e, NZL), rem(e, NZL), div(h, 2), rem(h, 2)
    jy, jx = div(j, 4), rem(j, 4)
    z = zh * NZL + zl
    core_peer = (e, zh * 2 + 1 - c)
    z8_peer = (e, (1 - zh) * 2 + c)

    def z_at(d):
        zz = rem(z + d, NZ)
        return div(zz, NZL), rem(zz, NZL)

    def z_dev(place):
        return (j * NZL + place[1], place[0] * 2 + c)

    def j_at(d):
        return rem(jy + div(d, 4), 4) * 4 + rem(jx + rem(d, 4), 4)

    def j_dev(jj):
        return (jj * NZL + zl, h)

    def rc(src, dst, ss, rs, dev):
        return pltpu.make_async_remote_copy(
            src_ref=src, dst_ref=dst, send_sem=ss, recv_sem=rs, device_id=dev, device_id_type=MESH
        )

    def each(n, body, start=1):
        lax.fori_loop(start, n, lambda k, carry: (body(k), carry)[1], 0)

    def far_first(k):
        return lax.select(rem(k, 2) == 1, 8 + div(k, 2), 8 - div(k, 2))

    barrier = pltpu.get_barrier_semaphore()
    pl.semaphore_signal(barrier, inc=1, device_id=core_peer, device_id_type=MESH)
    each(
        NZ,
        lambda k: pl.semaphore_signal(barrier, inc=1, device_id=z_dev(z_at(far_first(k))), device_id_type=MESH),
    )
    each(NJ, lambda d: pl.semaphore_signal(barrier, inc=1, device_id=j_dev(j_at(d)), device_id_type=MESH))
    w1_copy = pltpu.make_async_copy(w1_hbm, w1, wsem.at[0])
    w2_copy = pltpu.make_async_copy(w2_hbm, w2, wsem.at[1])
    w1_copy.start()
    w2_copy.start()

    mine, theirs = pl.ds(pl.multiple_of(c * HALF, 8), HALF), pl.ds(pl.multiple_of((1 - c) * HALF, 8), HALF)

    def laid_out(given, kept):
        for i in range(IMG):
            kept[i, TP - 16 : TP, :] = jnp.zeros((16, QF), BF16)
        whole = given[...].astype(F32)
        for i in range(IMG):
            kept[i, 0:TOK, :] = whole[:, i, :].astype(BF16)

    laid_out(tok_in, tok)
    for i in range(IMG):
        lp[i] = dot(tok[i], sp[...], 1, 0)
    pl.semaphore_wait(barrier, 1 + (NZ - 1) + (NJ - 1))

    def a1(i):
        return rc(lp.at[i, theirs], la.at[i], a1s.at[i], a1r.at[i], core_peer)

    def a2(i):
        return rc(lzs.at[i], lzr.at[i], a2s.at[i], a2r.at[i], z8_peer)

    def a3(i, rows):
        return rc(lf.at[i, rows], lf.at[i, rows], a3s.at[i], a3r.at[i], core_peer)

    def b1(i, t, src, dst, dev):
        return rc(s.at[i, t, src], r1.at[i, t, dst], b1s.at[i, t], b1r.at[i, t], dev)

    def b2(i, t, place):
        return rc(
            r2.at[i, t, place[1]], x.at[i, t, (zh * 2 + c) * NZL + zl], b2s.at[i, t], b2r.at[i, t], z_dev(place)
        )

    def fwd(i, t, half, core):
        there = x.at[i, t, pl.ds((half * 2 + core) * NZL, NZL)]
        return rc(there, there, fws.at[i, t, half], fwr.at[i, t, half], core_peer)

    def px(i, t):
        return rc(px_s.at[i, t], px_r.at[i, t], pxs.at[i, t], pxr.at[i, t], core_peer)

    def c1(i, t, place):
        return rc(cs.at[i, t, place[0] * NZL + place[1]], y.at[i, t, z], c1s.at[i, t], c1r.at[i, t], z_dev(place))

    def c2(i, t, dst, dev):
        return rc(q.at[i, t, dst], v.at[i, t, j], c2s.at[i, t], c2r.at[i, t], dev)

    fifteen = pl.ds(0, 15)

    def b1_all(i, t):
        return rc(s.at[i, t, fifteen], r1.at[i, t, fifteen], b1s.at[i, t], b1r.at[i, t], core_peer)

    def b2_all(i, t):
        return rc(x.at[i, t, fifteen], x.at[i, t, fifteen], b2s.at[i, t], b2r.at[i, t], core_peer)

    def c1_all(i, t):
        return rc(cs.at[i, t, fifteen], y.at[i, t, fifteen], c1s.at[i, t], c1r.at[i, t], core_peer)

    def c2_all(i, t):
        return rc(q.at[i, t, fifteen], v.at[i, t, fifteen], c2s.at[i, t], c2r.at[i, t], core_peer)

    def d1(i):
        return rc(gp.at[i, theirs], ga.at[i], d1s.at[i], d1r.at[i], core_peer)

    def d2(i):
        return rc(gzs.at[i], gzr.at[i], d2s.at[i], d2r.at[i], z8_peer)

    def d3(i, rows):
        return rc(gf.at[i, rows], gf.at[i, rows], d3s.at[i], d3r.at[i], core_peer)

    def logits_across(i):
        a1(i).wait_recv()
        lzs[i] = lp[i, mine] + la[i]
        a2(i).start()

    def logits_whole(i):
        a2(i).wait_recv()
        lf[i, mine] = lzs[i] + lzr[i]
        a3(i, mine).start()

    def send_slots(i, t):
        each(NJ, lambda d: b1(i, t, j_at(d), j, j_dev(j_at(d))).start())
        r1[i, t, j] = s[i, t, j]

    def dispatches(i):
        a3(i, theirs).wait_recv()
        row = lax.broadcasted_iota(jnp.int32, (TP, SLOTS), 0)
        masked = jnp.where(row < TOK, lf[i], -1e30)
        top = jnp.max(masked, axis=0, keepdims=True)
        up = jnp.exp(masked - top)
        dispatch = up / jnp.sum(up, axis=0, keepdims=True)
        disp[i] = dispatch
        dispatch_low = dispatch.astype(BF16)
        dlow[i] = dispatch_low
        s[i, 0] = dot(dispatch_low, tok[i], 0, 0).reshape(NJ, 8, QF).astype(BF16)
        send_slots(i, 0)

    def combines(i):
        logits = lf[i]
        top = jnp.max(logits, axis=1, keepdims=True)
        up = jnp.exp(logits - top)
        below = jnp.sum(up, axis=1, keepdims=True)
        combine = up / below
        comb[i] = combine
        combine_low = combine.astype(BF16)
        clow[i] = combine_low
        s[i, 1] = dot(combine_low, cot[i], 0, 0).reshape(NJ, 8, QF).astype(BF16)
        send_slots(i, 1)
        total = top + jnp.log(below)
        tcomb[i] = (2.0 * loss_weight) * total * combine
        wide = jnp.broadcast_to(loss_weight * total * total, (TP, SLOTS))
        zloss[i : i + 1, :] = jnp.transpose(wide)[0:1, 0:TOK]

    def to_experts(i, t):
        b1_all(i, t).wait_recv()
        rows = r1[i, t].astype(F32).reshape(SLOTS, QF)
        for lanes in range(2):
            fa[t, lanes] = rows[:, lanes * 128 : (lanes + 1) * 128]
        for low in range(NZL):
            rows = [fa[t, lanes, pl.ds(low, NJ, stride=8), :] for lanes in range(2)]
            r2[i, t, low] = jnp.concatenate(rows, axis=1).astype(BF16)
        each(NZ, lambda k: b2(i, t, z_at(far_first(k))).start())
        x[i, t, h * NZL + zl] = r2[i, t, zl]

    def arrive(i, t):
        b2_all(i, t).wait_recv()
        for half in range(2):
            fwd(i, t, half, c).start()

    def rows_of(i, t):
        for half in range(2):
            fwd(i, t, half, 1 - c).wait_recv()
        return jnp.concatenate(
            [x[i, t, k * NZL : (k + 1) * NZL].reshape(SLOTS, QF) for k in range(4)], axis=1
        )

    def quarter(k, core):
        return pl.ds(pl.multiple_of((k * 2 + core) * QF, QF), QF)

    FB = 256

    def expert_out(i):
        arrived = rows_of(i, 0)
        for f in range(0, 1024, FB):
            part = dot(arrived, w1[:, f : f + FB], 1, 0) + bi[:, f : f + FB].astype(F32)
            activated, slope_part = gelu_parts(part)
            act[0, :, f : f + FB] = activated.astype(BF16)
            slope[:, f : f + FB] = slope_part
        send_results(i, 0, lambda cols: dot(act[0], w2[:, cols], 1, 0))

    def expert_grad(i):
        arrived = rows_of(i, 1)
        for f in range(0, 1024, FB):
            part = dot(arrived, w2[f : f + FB, :], 1, 1) * slope[:, f : f + FB]
            act[1, :, f : f + FB] = part.astype(BF16)
        send_results(i, 1, lambda cols: dot(act[1], w1[cols, :], 1, 1))

    def send_results(i, t, product):
        for k in range(2):
            px_s[i, t, k] = product(quarter(k, 1 - c)).astype(BF16)
        px(i, t).start()
        own = [product(quarter(k, c)) for k in range(2)]
        px(i, t).wait_recv()
        for k in range(2):
            total = own[k] + px_r[i, t, k].astype(F32)
            if t == 0:
                total = total + jnp.where(zh == k, 1.0, 0.0) * bo[...].astype(F32)
            cs[i, t, k * NZL : (k + 1) * NZL] = total.reshape(NZL, NJ, QF).astype(BF16)
        each(NZ, lambda k: c1(i, t, z_at(far_first(k))).start())
        y[i, t, z] = cs[i, t, z]

    def to_images(i, t):
        c1_all(i, t).wait_recv()
        for low in range(NZL):
            rows = y[i, t, low].astype(F32) + y[i, t, NZL + low].astype(F32)
            for lanes in range(2):
                fb[t, lanes, pl.ds(low, NJ, stride=8), :] = rows[:, lanes * 128 : (lanes + 1) * 128]
        rows = jnp.concatenate([fb[t, lanes] for lanes in range(2)], axis=1)
        q[i, t] = rows.reshape(NJ, 8, QF).astype(BF16)
        each(NJ, lambda d: c2(i, t, j_at(d), j_dev(j_at(d))).start())
        v[i, t, j] = q[i, t, j]

    def back(i, t):
        return v[i, t].astype(F32).reshape(SLOTS, QF).astype(BF16)

    def outputs(i):
        c2_all(i, 0).wait_recv()
        slot_out = back(i, 0)
        mixed[i] = dot(clow[i], slot_out, 1, 0).astype(BF16)[0:TOK, :]
        combine_grad = dot(cot[i], slot_out, 1, 1)
        combine = comb[i]
        gp[i] = combine * (combine_grad - jnp.sum(combine * combine_grad, axis=1, keepdims=True))

    def gradients(i):
        c2_all(i, 1).wait_recv()
        dispatch_grad = dot(tok[i], back(i, 1), 1, 1)
        dispatch = disp[i]
        gp[i] += dispatch * (dispatch_grad - jnp.sum(dispatch * dispatch_grad, axis=0, keepdims=True))
        d1(i).start()

    def gradients_across(i):
        d1(i).wait_recv()
        half = gp[i, mine] + ga[i]
        gzs[i] = half.astype(BF16)
        d2(i).start()
        ga[i] = half + tcomb[i, mine]

    def gradients_whole(i):
        d2(i).wait_recv()
        half = ga[i] + gzr[i].astype(F32)
        gf[i, mine] = half.astype(BF16).astype(F32)
        d3(i, mine).start()

    def finish(i):
        result = dot(dlow[i], back(i, 1), 1, 0)
        d3(i, theirs).wait_recv()
        tgrad[i] = (result + dot(gf[i].astype(BF16), sp[...], 1, 1)).astype(BF16)[0:TOK, :]

    for copy in [a1(i) for i in range(IMG)]:
        copy.start()
    logits_across(0)
    logits_across(1)
    laid_out(cot_in, cot)
    logits_whole(0)
    dispatches(0)
    combines(0)
    logits_whole(1)
    to_experts(0, 0)
    to_experts(0, 1)
    dispatches(1)
    combines(1)
    to_experts(1, 0)
    to_experts(1, 1)
    w1_copy.wait()
    w2_copy.wait()
    arrive(0, 0)
    expert_out(0)
    arrive(0, 1)
    expert_grad(0)
    arrive(1, 0)
    expert_out(1)
    arrive(1, 1)
    expert_grad(1)
    to_images(0, 0)
    to_images(0, 1)
    outputs(0)
    gradients(0)
    gradients_across(0)
    to_images(1, 0)
    to_images(1, 1)
    outputs(1)
    gradients_whole(0)
    gradients(1)
    finish(0)
    gradients_across(1)
    gradients_whole(1)
    finish(1)

    for i in range(IMG):
        for copy in (a1(i), a2(i), a3(i, mine), d1(i), d2(i), d3(i, mine)):
            copy.wait_send()
        for t in range(2):
            for copy in (b1_all(i, t), b2_all(i, t), fwd(i, t, 0, c), fwd(i, t, 1, c)):
                copy.wait_send()
            for copy in (px(i, t), c1_all(i, t), c2_all(i, t)):
                copy.wait_send()


def per_device(tokens, slot_params, weight_in, bias_in, weight_out, bias_out, cotangent):
    vmem = pl.BlockSpec(memory_space=pltpu.VMEM)
    hbm = pl.BlockSpec(memory_space=pl.ANY)
    dma = pltpu.SemaphoreType.DMA
    scratch = [
        ((1024, 1024), BF16),
        ((1024, 1024), BF16),
        dma((2,)),
        ((IMG, TP, QF), BF16),
        ((IMG, TP, QF), BF16),
        ((IMG, TP, SLOTS), F32),
        ((IMG, HALF, SLOTS), F32),
        ((IMG, HALF, SLOTS), F32),
        ((IMG, HALF, SLOTS), F32),
        ((IMG, TP, SLOTS), F32),
        ((IMG, TP, SLOTS), F32),
        ((IMG, TP, SLOTS), F32),
        ((IMG, TP, SLOTS), F32),
        ((IMG, TP, SLOTS), BF16),
        ((IMG, TP, SLOTS), BF16),
        ((IMG, 2, NJ, 8, QF), BF16),
        ((IMG, 2, NJ, 8, QF), BF16),
        ((2, 2, SLOTS, 128), F32),
        ((IMG, 2, NZL, NJ, QF), BF16),
        ((IMG, 2, 4 * NZL, NJ, QF), BF16),
        ((2, SLOTS, 1024), BF16),
        ((SLOTS, 1024), F32),
        ((IMG, 2, 2, SLOTS, QF), BF16),
        ((IMG, 2, 2, SLOTS, QF), BF16),
        ((IMG, 2, NZ, NJ, QF), BF16),
        ((IMG, 2, NZ, NJ, QF), BF16),
        ((2, 2, SLOTS, 128), F32),
        ((IMG, 2, NJ, 8, QF), BF16),
        ((IMG, 2, NJ, 8, QF), BF16),
        ((IMG, TP, SLOTS), F32),
        ((IMG, HALF, SLOTS), F32),
        ((IMG, HALF, SLOTS), BF16),
        ((IMG, HALF, SLOTS), BF16),
        ((IMG, TP, SLOTS), F32),
    ]
    scratch = [pltpu.VMEM(*a) if isinstance(a, tuple) else a for a in scratch]
    scratch += [dma((IMG,))] * 6 + [dma((IMG, 2))] * 4 + [dma((IMG, 2, 2))] * 2 + [dma((IMG, 2))] * 6 + [dma((IMG,))] * 6
    return pl.pallas_call(
        kernel,
        out_shape=(
            jax.ShapeDtypeStruct((IMG, TOK, QF), BF16),
            jax.ShapeDtypeStruct((IMG, TOK, QF), BF16),
            jax.ShapeDtypeStruct((IMG, TOK), F32),
        ),
        in_specs=[vmem, vmem, hbm, vmem, hbm, vmem, vmem],
        out_specs=(vmem, vmem, vmem),
        scratch_shapes=scratch,
        compiler_params=pltpu.CompilerParams(
            collective_id=1, has_side_effects=True, vmem_limit_bytes=56 * 2**20
        ),
        name="layer",
    )(
        jnp.transpose(tokens, (1, 0, 2)),
        slot_params,
        weight_in.reshape(1024, 1024),
        bias_in,
        weight_out.reshape(1024, 1024),
        bias_out,
        jnp.transpose(cotangent, (1, 0, 2)),
    )


def solution(mesh):
    return jax.shard_map(
        per_device,
        mesh=mesh,
        in_specs=(
            P("expert", None, "hidden"),
            P("hidden", None),
            P("expert", None, "hidden"),
            P("expert", "hidden"),
            P("expert", "hidden", None),
            P("expert", "hidden"),
            P("expert", None, "hidden"),
        ),
        out_specs=(P("expert", None, "hidden"), P("expert", None, "hidden"), P("expert", None)),
        check_vma=False,
    )
```

time: 116 us -> 105 us (0.905)
  Pallas kernels: 107 us -> 99.6 us
  local copies, waits for them, and re-layouts: 8.16 us -> 4.77 us
    pallas_call x1, Pallas kernels: 107 us -> 99.6 us  [per_device(): pl.pallas_call(kernel, out_shape=(jax.ShapeDtypeStruct((IMG, TOK, QF), BF...]
    pallas_call x0 -> x2, local copies, waits for them, and re-layouts: none -> 3.53 us  [per_device(): pl.pallas_call(kernel, out_shape=(jax.ShapeDtypeStruct((IMG, TOK, QF), BF...]
    unnamed x5 -> x1, local copies, waits for them, and re-layouts: 4.15 us -> 1.24 us
    slice x3 -> x0, local copies, waits for them, and re-layouts: 2.61 us -> none  [per_device(): return (mixed[:, :TOK], token_grad[:, :TOK], zloss[:, 0, :TOK])]
    pad x2 -> x0, local copies, waits for them, and re-layouts: 1.4 us -> none  [the longest x1 0.71 us: per_device(): jnp.pad(cotangent, pad)]
where the time goes in v2:
time: 105 us
  Pallas kernels  99.6 us (95%)
  local copies, waits for them, and re-layouts  4.77 us (5%)
    pallas_call x1, Pallas kernels, per_device(): pl.pallas_call(kernel, out_shape=(jax.ShapeDtypeStruct((IMG, TOK, QF), BF...  99.6 us
    pallas_call x2, local copies, waits for them, and re-layouts, per_device(): pl.pallas_call(kernel, out_shape=(jax.ShapeDtypeStruct((IMG, TOK, QF), BF...  3.53 us

profile of v2, /device:TPU:1, one launch (start us, length us, event | category | flops | bytes accessed | tf_op | source)
XLA Modules:
  0.0 105.0 jit_solution(938494505975087893)
XLA Ops:
  0.6 99.6 %layer.1 = (bf16[2,196,256]{2,1,0:T(8,128)(2,1)}, bf16[2,196,256]{2,1,0:T(8,128)(2,1)}, f32[2,196]{1,0:T(2,128)}) custom-call(bf16[196,2,256]{2,1,0:T(2,128)(2,1)} %bitcast.6, bf16[256,128]{1,0:T(8,128)(2,1)} %sp.1, bf16[1024,1024]{1,0:T(8,128)(2,1)} %bitcast.4, bf16[1,1024]{1,0:T(2,128)(2,1)} %bi.1, bf16[1024,1024]{1,0:T(8,128)(2,1)} %bitcast.5, ...), custom_call_target="tpu_custom_call" | custom-call | tf_op jit(solution)/shard_map/layer/pallas_call | solution.py:394
  100.2 1.8 %copy.10 = bf16[2,196,256]{2,0,1:T(2,128)(2,1)} copy(bf16[2,196,256]{2,1,0:T(8,128)(2,1)} %get-tuple-element.3) | data formatting | bytes 401408 | tf_op jit(solution)/shard_map/layer/pallas_call | solution.py:394
  102.0 1.8 %copy.11 = bf16[2,196,256]{2,0,1:T(2,128)(2,1)} copy(bf16[2,196,256]{2,1,0:T(8,128)(2,1)} %get-tuple-element.4) | data formatting | bytes 401408 | tf_op jit(solution)/shard_map/layer/pallas_call | solution.py:394
  103.8 1.2 %copy.13 = f32[2,196]{1,0:T(2,128)} copy(f32[2,196]{1,0:T(2,128)} %get-tuple-element.11) | data formatting | bytes 3136

commit v3 on v2

--- a/solution.py
+++ b/solution.py
@@ -29,13 +29,13 @@
 
 
 def kernel(
-    tok_in, sp, w1_hbm, bi, w2_hbm, bo, cot_in,
+    tok_hbm, sp_hbm, w1_hbm, bi_hbm, w2_hbm, bo_hbm, cot_hbm,
     mixed, tgrad, zloss,
-    w1, w2, wsem, tok, cot,
+    tok_in, sp, w1, bi, w2, bo, cot_in, insem, tok, cot,
     lp, la, lzs, lzr, lf,
     disp, comb, tcomb, dlow, clow,
     s, r1, fa, r2, x,
-    act, slope, px_s, px_r, cs, y, fb, q, v,
+    act, slope, part, px_s, px_r, ft, cq, cr, fc, cs, y, fb, v,
     gp, ga, gzs, gzr, gf,
     a1s, a1r, a2s, a2r, a3s, a3r, b1s, b1r, b2s, b2r, fws, fwr,
     pxs, pxr, c1s, c1r, c2s, c2r, d1s, d1r, d2s, d2r, d3s, d3r,
@@ -79,10 +79,11 @@
         lambda k: pl.semaphore_signal(barrier, inc=1, device_id=z_dev(z_at(far_first(k))), device_id_type=MESH),
     )
     each(NJ, lambda d: pl.semaphore_signal(barrier, inc=1, device_id=j_dev(j_at(d)), device_id_type=MESH))
-    w1_copy = pltpu.make_async_copy(w1_hbm, w1, wsem.at[0])
-    w2_copy = pltpu.make_async_copy(w2_hbm, w2, wsem.at[1])
-    w1_copy.start()
-    w2_copy.start()
+    given = (tok_hbm, sp_hbm, cot_hbm, w1_hbm, bi_hbm, w2_hbm, bo_hbm)
+    kept = (tok_in, sp, cot_in, w1, bi, w2, bo)
+    loads = [pltpu.make_async_copy(a, b, insem.at[k]) for k, (a, b) in enumerate(zip(given, kept))]
+    for load in loads:
+        load.start()
 
     mine, theirs = pl.ds(pl.multiple_of(c * HALF, 8), HALF), pl.ds(pl.multiple_of((1 - c) * HALF, 8), HALF)
 
@@ -93,7 +94,9 @@
         for i in range(IMG):
             kept[i, 0:TOK, :] = whole[:, i, :].astype(BF16)
 
+    loads[0].wait()
     laid_out(tok_in, tok)
+    loads[1].wait()
     for i in range(IMG):
         lp[i] = dot(tok[i], sp[...], 1, 0)
     pl.semaphore_wait(barrier, 1 + (NZ - 1) + (NJ - 1))
@@ -122,11 +125,11 @@
     def px(i, t):
         return rc(px_s.at[i, t], px_r.at[i, t], pxs.at[i, t], pxr.at[i, t], core_peer)
 
-    def c1(i, t, place):
-        return rc(cs.at[i, t, place[0] * NZL + place[1]], y.at[i, t, z], c1s.at[i, t], c1r.at[i, t], z_dev(place))
-
-    def c2(i, t, dst, dev):
-        return rc(q.at[i, t, dst], v.at[i, t, j], c2s.at[i, t], c2r.at[i, t], dev)
+    def c1(i, t, dst, dev):
+        return rc(cq.at[i, t, dst], cr.at[i, t, j], c1s.at[i, t], c1r.at[i, t], dev)
+
+    def c2(i, t, place):
+        return rc(cs.at[i, t, place[0] * NZL + place[1]], y.at[i, t, z], c2s.at[i, t], c2r.at[i, t], z_dev(place))
 
     fifteen = pl.ds(0, 15)
 
@@ -137,10 +140,10 @@
         return rc(x.at[i, t, fifteen], x.at[i, t, fifteen], b2s.at[i, t], b2r.at[i, t], core_peer)
 
     def c1_all(i, t):
-        return rc(cs.at[i, t, fifteen], y.at[i, t, fifteen], c1s.at[i, t], c1r.at[i, t], core_peer)
+        return rc(cq.at[i, t, fifteen], cr.at[i, t, fifteen], c1s.at[i, t], c1r.at[i, t], core_peer)
 
     def c2_all(i, t):
-        return rc(q.at[i, t, fifteen], v.at[i, t, fifteen], c2s.at[i, t], c2r.at[i, t], core_peer)
+        return rc(cs.at[i, t, fifteen], y.at[i, t, fifteen], c2s.at[i, t], c2r.at[i, t], core_peer)
 
     def d1(i):
         return rc(gp.at[i, theirs], ga.at[i], d1s.at[i], d1r.at[i], core_peer)
@@ -210,32 +213,40 @@
         for half in range(2):
             fwd(i, t, half, c).start()
 
-    def rows_of(i, t):
+    def quarter(k, core):
+        return pl.ds(pl.multiple_of((k * 2 + core) * QF, QF), QF)
+
+    FB = 256
+
+    def by_features(i, t, core, product):
+        arrived = [x[i, t, pl.ds((k * 2 + core) * NZL, NZL)].reshape(SLOTS, QF) for k in range(2)]
+        for f in range(0, 1024, FB):
+            yield f, sum(product(arrived[k], quarter(k, core), f) for k in range(2))
+
+    def project(i, t, product):
+        for f, total in by_features(i, t, c, product):
+            part[:, f : f + FB] = total
         for half in range(2):
             fwd(i, t, half, 1 - c).wait_recv()
-        return jnp.concatenate(
-            [x[i, t, k * NZL : (k + 1) * NZL].reshape(SLOTS, QF) for k in range(4)], axis=1
-        )
-
-    def quarter(k, core):
-        return pl.ds(pl.multiple_of((k * 2 + core) * QF, QF), QF)
-
-    FB = 256
+        for f, total in by_features(i, t, 1 - c, product):
+            yield f, part[:, f : f + FB] + total
 
     def expert_out(i):
-        arrived = rows_of(i, 0)
-        for f in range(0, 1024, FB):
-            part = dot(arrived, w1[:, f : f + FB], 1, 0) + bi[:, f : f + FB].astype(F32)
-            activated, slope_part = gelu_parts(part)
+        def product(rows, features, f):
+            return dot(rows, w1[features, f : f + FB], 1, 0)
+
+        for f, total in project(i, 0, product):
+            activated, slope_part = gelu_parts(total + bi[:, f : f + FB].astype(F32))
             act[0, :, f : f + FB] = activated.astype(BF16)
             slope[:, f : f + FB] = slope_part
         send_results(i, 0, lambda cols: dot(act[0], w2[:, cols], 1, 0))
 
     def expert_grad(i):
-        arrived = rows_of(i, 1)
-        for f in range(0, 1024, FB):
-            part = dot(arrived, w2[f : f + FB, :], 1, 1) * slope[:, f : f + FB]
-            act[1, :, f : f + FB] = part.astype(BF16)
+        def product(rows, features, f):
+            return dot(rows, w2[f : f + FB, features], 1, 1)
+
+        for f, total in project(i, 1, product):
+            act[1, :, f : f + FB] = (total * slope[:, f : f + FB]).astype(BF16)
         send_results(i, 1, lambda cols: dot(act[1], w1[cols, :], 1, 1))
 
     def send_results(i, t, product):
@@ -248,35 +259,45 @@
             total = own[k] + px_r[i, t, k].astype(F32)
             if t == 0:
                 total = total + jnp.where(zh == k, 1.0, 0.0) * bo[...].astype(F32)
-            cs[i, t, k * NZL : (k + 1) * NZL] = total.reshape(NZL, NJ, QF).astype(BF16)
-        each(NZ, lambda k: c1(i, t, z_at(far_first(k))).start())
+            for lanes in range(2):
+                ft[k, lanes] = total[:, lanes * 128 : (lanes + 1) * 128]
+        for dst in range(NJ):
+            for k in range(2):
+                rows = [ft[k, lanes, pl.ds(dst, 8, stride=NJ), :] for lanes in range(2)]
+                cq[i, t, dst, k] = jnp.concatenate(rows, axis=1).astype(BF16)
+        each(NJ, lambda d: c1(i, t, j_at(d), j_dev(j_at(d))).start())
+        cr[i, t, j] = cq[i, t, j]
+
+    def turn(i, t):
+        c1_all(i, t).wait_recv()
+        for k in range(2):
+            rows = cr[i, t, :, k].astype(F32).reshape(SLOTS, QF)
+            for lanes in range(2):
+                fc[k, lanes] = rows[:, lanes * 128 : (lanes + 1) * 128]
+        for k in range(2):
+            for low in range(NZL):
+                rows = [fc[k, lanes, pl.ds(low, NJ, stride=8), :] for lanes in range(2)]
+                cs[i, t, k * NZL + low] = jnp.concatenate(rows, axis=1).astype(BF16)
+        each(NZ, lambda k: c2(i, t, z_at(far_first(k))).start())
         y[i, t, z] = cs[i, t, z]
 
-    def to_images(i, t):
-        c1_all(i, t).wait_recv()
+    def home(i, t):
+        c2_all(i, t).wait_recv()
         for low in range(NZL):
             rows = y[i, t, low].astype(F32) + y[i, t, NZL + low].astype(F32)
             for lanes in range(2):
-                fb[t, lanes, pl.ds(low, NJ, stride=8), :] = rows[:, lanes * 128 : (lanes + 1) * 128]
-        rows = jnp.concatenate([fb[t, lanes] for lanes in range(2)], axis=1)
-        q[i, t] = rows.reshape(NJ, 8, QF).astype(BF16)
-        each(NJ, lambda d: c2(i, t, j_at(d), j_dev(j_at(d))).start())
-        v[i, t, j] = q[i, t, j]
-
-    def back(i, t):
-        return v[i, t].astype(F32).reshape(SLOTS, QF).astype(BF16)
+                fb[lanes, pl.ds(low, NJ, stride=8), :] = rows[:, lanes * 128 : (lanes + 1) * 128]
+        v[i, t] = jnp.concatenate([fb[lanes] for lanes in range(2)], axis=1).astype(BF16)
 
     def outputs(i):
-        c2_all(i, 0).wait_recv()
-        slot_out = back(i, 0)
+        slot_out = v[i, 0]
         mixed[i] = dot(clow[i], slot_out, 1, 0).astype(BF16)[0:TOK, :]
         combine_grad = dot(cot[i], slot_out, 1, 1)
         combine = comb[i]
         gp[i] = combine * (combine_grad - jnp.sum(combine * combine_grad, axis=1, keepdims=True))
 
     def gradients(i):
-        c2_all(i, 1).wait_recv()
-        dispatch_grad = dot(tok[i], back(i, 1), 1, 1)
+        dispatch_grad = dot(tok[i], v[i, 1], 1, 1)
         dispatch = disp[i]
         gp[i] += dispatch * (dispatch_grad - jnp.sum(dispatch * dispatch_grad, axis=0, keepdims=True))
         d1(i).start()
@@ -295,7 +316,7 @@
         d3(i, mine).start()
 
     def finish(i):
-        result = dot(dlow[i], back(i, 1), 1, 0)
+        result = dot(dlow[i], v[i, 1], 1, 0)
         d3(i, theirs).wait_recv()
         tgrad[i] = (result + dot(gf[i].astype(BF16), sp[...], 1, 1)).astype(BF16)[0:TOK, :]
 
@@ -303,6 +324,7 @@
         copy.start()
     logits_across(0)
     logits_across(1)
+    loads[2].wait()
     laid_out(cot_in, cot)
     logits_whole(0)
     dispatches(0)
@@ -314,49 +336,59 @@
     combines(1)
     to_experts(1, 0)
     to_experts(1, 1)
-    w1_copy.wait()
-    w2_copy.wait()
+    for load in loads[3:]:
+        load.wait()
     arrive(0, 0)
     expert_out(0)
     arrive(0, 1)
     expert_grad(0)
+    turn(0, 0)
     arrive(1, 0)
     expert_out(1)
+    turn(0, 1)
     arrive(1, 1)
     expert_grad(1)
-    to_images(0, 0)
-    to_images(0, 1)
+    turn(1, 0)
+    turn(1, 1)
+    home(0, 0)
     outputs(0)
+    home(0, 1)
     gradients(0)
     gradients_across(0)
-    to_images(1, 0)
-    to_images(1, 1)
+    home(1, 0)
     outputs(1)
+    home(1, 1)
+    gradients(1)
+    gradients_across(1)
     gradients_whole(0)
-    gradients(1)
     finish(0)
-    gradients_across(1)
-    gradients_whole(1)
-    finish(1)
-
     for i in range(IMG):
-        for copy in (a1(i), a2(i), a3(i, mine), d1(i), d2(i), d3(i, mine)):
+        for copy in (a1(i), a2(i), a3(i, mine), d1(i), d2(i)):
             copy.wait_send()
         for t in range(2):
             for copy in (b1_all(i, t), b2_all(i, t), fwd(i, t, 0, c), fwd(i, t, 1, c)):
                 copy.wait_send()
             for copy in (px(i, t), c1_all(i, t), c2_all(i, t)):
                 copy.wait_send()
+    gradients_whole(1)
+    finish(1)
+    d3(0, mine).wait_send()
+    d3(1, mine).wait_send()
 
 
 def per_device(tokens, slot_params, weight_in, bias_in, weight_out, bias_out, cotangent):
     vmem = pl.BlockSpec(memory_space=pltpu.VMEM)
-    hbm = pl.BlockSpec(memory_space=pl.ANY)
+    hbm = pl.BlockSpec(memory_space=pltpu.HBM)
     dma = pltpu.SemaphoreType.DMA
     scratch = [
+        ((TOK, IMG, QF), BF16),
+        ((QF, SLOTS), BF16),
         ((1024, 1024), BF16),
+        ((1, 1024), BF16),
         ((1024, 1024), BF16),
-        dma((2,)),
+        ((1, QF), BF16),
+        ((TOK, IMG, QF), BF16),
+        dma((7,)),
         ((IMG, TP, QF), BF16),
         ((IMG, TP, QF), BF16),
         ((IMG, TP, SLOTS), F32),
@@ -376,13 +408,17 @@
         ((IMG, 2, 4 * NZL, NJ, QF), BF16),
         ((2, SLOTS, 1024), BF16),
         ((SLOTS, 1024), F32),
+        ((SLOTS, 1024), F32),
         ((IMG, 2, 2, SLOTS, QF), BF16),
         ((IMG, 2, 2, SLOTS, QF), BF16),
+        ((2, 2, SLOTS, 128), F32),
+        ((IMG, 2, NJ, 2, 8, QF), BF16),
+        ((IMG, 2, NJ, 2, 8, QF), BF16),
+        ((2, 2, SLOTS, 128), F32),
         ((IMG, 2, NZ, NJ, QF), BF16),
         ((IMG, 2, NZ, NJ, QF), BF16),
-        ((2, 2, SLOTS, 128), F32),
-        ((IMG, 2, NJ, 8, QF), BF16),
-        ((IMG, 2, NJ, 8, QF), BF16),
+        ((2, SLOTS, 128), F32),
+        ((IMG, 2, SLOTS, QF), BF16),
         ((IMG, TP, SLOTS), F32),
         ((IMG, HALF, SLOTS), F32),
         ((IMG, HALF, SLOTS), BF16),
@@ -398,21 +434,26 @@
             jax.ShapeDtypeStruct((IMG, TOK, QF), BF16),
             jax.ShapeDtypeStruct((IMG, TOK), F32),
         ),
-        in_specs=[vmem, vmem, hbm, vmem, hbm, vmem, vmem],
+        in_specs=[hbm] * 7,
         out_specs=(vmem, vmem, vmem),
         scratch_shapes=scratch,
         compiler_params=pltpu.CompilerParams(
-            collective_id=1, has_side_effects=True, vmem_limit_bytes=56 * 2**20
+            collective_id=1, has_side_effects=True, vmem_limit_bytes=20 * 2**20
         ),
         name="layer",
     )(
-        jnp.transpose(tokens, (1, 0, 2)),
-        slot_params,
-        weight_in.reshape(1024, 1024),
-        bias_in,
-        weight_out.reshape(1024, 1024),
-        bias_out,
-        jnp.transpose(cotangent, (1, 0, 2)),
+        *(
+            pltpu.with_memory_space_constraint(given, pltpu.HBM)
+            for given in (
+                jnp.transpose(tokens, (1, 0, 2)),
+                slot_params,
+                weight_in.reshape(1024, 1024),
+                bias_in,
+                weight_out.reshape(1024, 1024),
+                bias_out,
+                jnp.transpose(cotangent, (1, 0, 2)),
+            )
+        )
     )
 
 

time: 105 us -> 94.2 us (0.90)
  Pallas kernels: 99.6 us -> 91.2 us
  local copies, waits for them, and re-layouts: 4.77 us -> 2.24 us
    pallas_call x1, Pallas kernels: 99.6 us -> 91.2 us  [per_device(): pl.pallas_call(kernel, out_shape=(jax.ShapeDtypeStruct((IMG, TOK, QF), BF...]
    pallas_call x2, local copies, waits for them, and re-layouts: 3.53 us -> 1.67 us  [per_device(): pl.pallas_call(kernel, out_shape=(jax.ShapeDtypeStruct((IMG, TOK, QF), BF...]
where the time goes in v3:
time: 94.2 us; the launch traced here: 94.1 us
  Pallas kernels  91.2 us (97%)
  local copies, waits for them, and re-layouts  2.24 us (2%)
    pallas_call x1, Pallas kernels, per_device(): pl.pallas_call(kernel, out_shape=(jax.ShapeDtypeStruct((IMG, TOK, QF), BF...  91.2 us

profile of v3, /device:TPU:1, one launch (start us, length us, event | category | flops | bytes accessed | tf_op | source)
XLA Modules:
  0.0 94.1 jit_solution(5243715384185304727)
XLA Ops:
  0.6 91.2 %layer.1 = (bf16[2,196,256]{2,1,0:T(8,128)(2,1)S(1)}, bf16[2,196,256]{2,1,0:T(8,128)(2,1)S(1)}, f32[2,196]{1,0:T(2,128)S(1)}) custom-call(bf16[196,2,256]{2,1,0:T(2,128)(2,1)} %bitcast.6, bf16[256,128]{1,0:T(8,128)(2,1)} %sp_hbm.1, bf16[1024,1024]{1,0:T(8,128)(2,1)} %bitcast.4, bf16[1,1024]{1,0:T(2,128)(2,1)} %bi_hbm.1, bf16[1024,1024]{1,0:T(8,128)(2,1)} %bitcast.5, ...), custom_call_target="tpu_custom_call" | custom-call | tf_op jit(solution)/shard_map/layer/pallas_call | solution.py:430
  91.8 0.8 copy.10
  92.6 0.8 copy.11
  93.5 0.6 copy.13

commit v4 on v3

--- a/solution.py
+++ b/solution.py
@@ -56,7 +56,7 @@
         return (j * NZL + place[1], place[0] * 2 + c)
 
     def j_at(d):
-        return rem(jy + div(d, 4), 4) * 4 + rem(jx + rem(d, 4), 4)
+        return rem(jy + d // 4, 4) * 4 + rem(jx + d % 4, 4)
 
     def j_dev(jj):
         return (jj * NZL + zl, h)
@@ -66,23 +66,28 @@
             src_ref=src, dst_ref=dst, send_sem=ss, recv_sem=rs, device_id=dev, device_id_type=MESH
         )
 
-    def each(n, body, start=1):
-        lax.fori_loop(start, n, lambda k, carry: (body(k), carry)[1], 0)
-
-    def far_first(k):
-        return lax.select(rem(k, 2) == 1, 8 + div(k, 2), 8 - div(k, 2))
+    along_z = (8, 7, 9, 6, 10, 5, 11, 4, 12, 3, 13, 2, 14, 1, 15)
+    in_plane = (10, 6, 14, 9, 11, 5, 7, 13, 15, 2, 8, 1, 3, 4, 12)
+
+    def each(steps, body):
+        for d in steps:
+            body(d)
 
     barrier = pltpu.get_barrier_semaphore()
-    pl.semaphore_signal(barrier, inc=1, device_id=core_peer, device_id_type=MESH)
-    each(
-        NZ,
-        lambda k: pl.semaphore_signal(barrier, inc=1, device_id=z_dev(z_at(far_first(k))), device_id_type=MESH),
-    )
-    each(NJ, lambda d: pl.semaphore_signal(barrier, inc=1, device_id=j_dev(j_at(d)), device_id_type=MESH))
+
+    def greet(dev):
+        pl.semaphore_signal(barrier, inc=1, device_id=dev, device_id_type=MESH)
+
     given = (tok_hbm, sp_hbm, cot_hbm, w1_hbm, bi_hbm, w2_hbm, bo_hbm)
     kept = (tok_in, sp, cot_in, w1, bi, w2, bo)
     loads = [pltpu.make_async_copy(a, b, insem.at[k]) for k, (a, b) in enumerate(zip(given, kept))]
-    for load in loads:
+    greet(z8_peer)
+    loads[0].start()
+    loads[1].start()
+    each(along_z[1:], lambda d: greet(z_dev(z_at(d))))
+    each(in_plane, lambda d: greet(j_dev(j_at(d))))
+    greet(core_peer)
+    for load in loads[2:]:
         load.start()
 
     mine, theirs = pl.ds(pl.multiple_of(c * HALF, 8), HALF), pl.ds(pl.multiple_of((1 - c) * HALF, 8), HALF)
@@ -157,15 +162,18 @@
     def logits_across(i):
         a1(i).wait_recv()
         lzs[i] = lp[i, mine] + la[i]
-        a2(i).start()
+        if i == 0:
+            a2(i).start()
 
     def logits_whole(i):
         a2(i).wait_recv()
         lf[i, mine] = lzs[i] + lzr[i]
         a3(i, mine).start()
+        if i == 0:
+            a2(1).start()
 
     def send_slots(i, t):
-        each(NJ, lambda d: b1(i, t, j_at(d), j, j_dev(j_at(d))).start())
+        each(in_plane, lambda d: b1(i, t, j_at(d), j, j_dev(j_at(d))).start())
         r1[i, t, j] = s[i, t, j]
 
     def dispatches(i):
@@ -205,7 +213,7 @@
         for low in range(NZL):
             rows = [fa[t, lanes, pl.ds(low, NJ, stride=8), :] for lanes in range(2)]
             r2[i, t, low] = jnp.concatenate(rows, axis=1).astype(BF16)
-        each(NZ, lambda k: b2(i, t, z_at(far_first(k))).start())
+        each(along_z, lambda k: b2(i, t, z_at(k)).start())
         x[i, t, h * NZL + zl] = r2[i, t, zl]
 
     def arrive(i, t):
@@ -265,7 +273,7 @@
             for k in range(2):
                 rows = [ft[k, lanes, pl.ds(dst, 8, stride=NJ), :] for lanes in range(2)]
                 cq[i, t, dst, k] = jnp.concatenate(rows, axis=1).astype(BF16)
-        each(NJ, lambda d: c1(i, t, j_at(d), j_dev(j_at(d))).start())
+        each(in_plane, lambda d: c1(i, t, j_at(d), j_dev(j_at(d))).start())
         cr[i, t, j] = cq[i, t, j]
 
     def turn(i, t):
@@ -278,7 +286,7 @@
             for low in range(NZL):
                 rows = [fc[k, lanes, pl.ds(low, NJ, stride=8), :] for lanes in range(2)]
                 cs[i, t, k * NZL + low] = jnp.concatenate(rows, axis=1).astype(BF16)
-        each(NZ, lambda k: c2(i, t, z_at(far_first(k))).start())
+        each(along_z, lambda k: c2(i, t, z_at(k)).start())
         y[i, t, z] = cs[i, t, z]
 
     def home(i, t):
@@ -329,9 +337,9 @@
     logits_whole(0)
     dispatches(0)
     combines(0)
-    logits_whole(1)
     to_experts(0, 0)
     to_experts(0, 1)
+    logits_whole(1)
     dispatches(1)
     combines(1)
     to_experts(1, 0)
@@ -376,6 +384,13 @@
     d3(1, mine).wait_send()
 
 
+def deliver(mixed_in, tgrad_in, zloss_in, mixed, tgrad, zloss):
+    for given, wanted in ((mixed_in, mixed), (tgrad_in, tgrad)):
+        both = [given[i].astype(F32) for i in range(IMG)]
+        wanted[...] = jnp.stack(both, axis=1).astype(BF16)
+    zloss[...] = zloss_in[...]
+
+
 def per_device(tokens, slot_params, weight_in, bias_in, weight_out, bias_out, cotangent):
     vmem = pl.BlockSpec(memory_space=pltpu.VMEM)
     hbm = pl.BlockSpec(memory_space=pltpu.HBM)
@@ -427,7 +442,7 @@
     ]
     scratch = [pltpu.VMEM(*a) if isinstance(a, tuple) else a for a in scratch]
     scratch += [dma((IMG,))] * 6 + [dma((IMG, 2))] * 4 + [dma((IMG, 2, 2))] * 2 + [dma((IMG, 2))] * 6 + [dma((IMG,))] * 6
-    return pl.pallas_call(
+    done = pl.pallas_call(
         kernel,
         out_shape=(
             jax.ShapeDtypeStruct((IMG, TOK, QF), BF16),
@@ -455,6 +470,19 @@
             )
         )
     )
+    mixed, token_grad, zloss = pl.pallas_call(
+        deliver,
+        out_shape=(
+            jax.ShapeDtypeStruct((TOK, IMG, QF), BF16),
+            jax.ShapeDtypeStruct((TOK, IMG, QF), BF16),
+            jax.ShapeDtypeStruct((IMG, TOK), F32),
+        ),
+        in_specs=[vmem] * 3,
+        out_specs=(vmem, vmem, vmem),
+        compiler_params=pltpu.CompilerParams(vmem_limit_bytes=20 * 2**20),
+        name="deliver",
+    )(*done)
+    return jnp.transpose(mixed, (1, 0, 2)), jnp.transpose(token_grad, (1, 0, 2)), zloss
 
 
 def solution(mesh):

time: 94.2 us -> 93.2 us (0.989)
  local copies, waits for them, and re-layouts: 2.24 us -> 0 us
  Pallas kernels: 91.2 us -> 92.4 us
    pallas_call x2 -> x0, local copies, waits for them, and re-layouts: 1.67 us -> none  [per_device(): pl.pallas_call(kernel, out_shape=(jax.ShapeDtypeStruct((IMG, TOK, QF), BF...]
    pallas_call x0 -> x1, Pallas kernels: none -> 1.31 us  [per_device(): pl.pallas_call(deliver, out_shape=(jax.ShapeDtypeStruct((TOK, IMG, QF), B...]
where the time goes in v4:
time: 93.2 us; the launch traced here: 93 us
  Pallas kernels  92.4 us (99%)
    pallas_call x1, Pallas kernels, per_device(): pl.pallas_call(kernel, out_shape=(jax.ShapeDtypeStruct((IMG, TOK, QF), BF...  91.1 us

profile of v4, /device:TPU:1, one launch (start us, length us, event | category | flops | bytes accessed | tf_op | source)
XLA Modules:
  0.0 93.0 jit_solution(9186277613416303490)
XLA Ops:
  0.6 91.1 %layer.1 = (bf16[2,196,256]{2,1,0:T(8,128)(2,1)S(1)}, bf16[2,196,256]{2,1,0:T(8,128)(2,1)S(1)}, f32[2,196]{1,0:T(2,128)S(1)}) custom-call(bf16[196,2,256]{2,1,0:T(2,128)(2,1)} %bitcast.8, bf16[256,128]{1,0:T(8,128)(2,1)} %sp_hbm.1, bf16[1024,1024]{1,0:T(8,128)(2,1)} %bitcast.6, bf16[1,1024]{1,0:T(2,128)(2,1)} %bi_hbm.1, bf16[1024,1024]{1,0:T(8,128)(2,1)} %bitcast.7, ...), custom_call_target="tpu_custom_call" | custom-call | tf_op jit(solution)/shard_map/layer/pallas_call | solution.py:445
  91.7 1.3 %deliver.1 = (bf16[196,2,256]{2,1,0:T(2,128)(2,1)}, bf16[196,2,256]{2,1,0:T(2,128)(2,1)}, f32[2,196]{1,0:T(2,128)}) custom-call(bf16[2,196,256]{2,1,0:T(8,128)(2,1)S(1)} %get-tuple-element.9.mixed_in, bf16[2,196,256]{2,1,0:T(8,128)(2,1)S(1)} %get-tuple-element.10.tgrad_in, f32[2,196]{1,0:T(2,128)S(1)} %get-tuple-element.11.zloss_in), custom_call_target="tpu_custom_call" | custom-call | tf_op jit(solution)/shard_map/deliver/pallas_call | solution.py:473

commit v5 on v4

--- a/solution.py
+++ b/solution.py
@@ -34,7 +34,7 @@
     tok_in, sp, w1, bi, w2, bo, cot_in, insem, tok, cot,
     lp, la, lzs, lzr, lf,
     disp, comb, tcomb, dlow, clow,
-    s, r1, fa, r2, x,
+    s, r1, fa, r2, x, wz, fw, xs, x0,
     act, slope, part, px_s, px_r, ft, cq, cr, fc, cs, y, fb, v,
     gp, ga, gzs, gzr, gf,
     a1s, a1r, a2s, a2r, a3s, a3r, b1s, b1r, b2s, b2r, fws, fwr,
@@ -115,16 +115,18 @@
     def a3(i, rows):
         return rc(lf.at[i, rows], lf.at[i, rows], a3s.at[i], a3r.at[i], core_peer)
 
-    def b1(i, t, src, dst, dev):
-        return rc(s.at[i, t, src], r1.at[i, t, dst], b1s.at[i, t], b1r.at[i, t], dev)
+    def b1(i, t, dst, dev):
+        out, into = (s.at[i, t, dst], r1.at[i, t, j]) if i else (xs.at[t, dst], x0.at[t, 0, j])
+        return rc(out, into, b1s.at[i, t], b1r.at[i, t], dev)
 
     def b2(i, t, place):
-        return rc(
-            r2.at[i, t, place[1]], x.at[i, t, (zh * 2 + c) * NZL + zl], b2s.at[i, t], b2r.at[i, t], z_dev(place)
-        )
+        into = x.at[t, (zh * 2 + c) * NZL + zl] if i else wz.at[t, z]
+        return rc(r2.at[i, t, place[1]], into, b2s.at[i, t], b2r.at[i, t], z_dev(place))
 
     def fwd(i, t, half, core):
-        there = x.at[i, t, pl.ds((half * 2 + core) * NZL, NZL)]
+        if i == 0:
+            return rc(x0.at[t, 0, :, half], x0.at[t, 1, :, half], fws.at[i, t, half], fwr.at[i, t, half], core_peer)
+        there = x.at[t, pl.ds((half * 2 + core) * NZL, NZL)]
         return rc(there, there, fws.at[i, t, half], fwr.at[i, t, half], core_peer)
 
     def px(i, t):
@@ -139,10 +141,12 @@
     fifteen = pl.ds(0, 15)
 
     def b1_all(i, t):
-        return rc(s.at[i, t, fifteen], r1.at[i, t, fifteen], b1s.at[i, t], b1r.at[i, t], core_peer)
+        out, into = (s.at[i, t], r1.at[i, t]) if i else (xs.at[t], x0.at[t, 0])
+        return rc(out.at[fifteen], into.at[fifteen], b1s.at[i, t], b1r.at[i, t], core_peer)
 
     def b2_all(i, t):
-        return rc(x.at[i, t, fifteen], x.at[i, t, fifteen], b2s.at[i, t], b2r.at[i, t], core_peer)
+        into = x.at[t, fifteen] if i else wz.at[t, fifteen]
+        return rc(into, into, b2s.at[i, t], b2r.at[i, t], core_peer)
 
     def c1_all(i, t):
         return rc(cq.at[i, t, fifteen], cr.at[i, t, fifteen], c1s.at[i, t], c1r.at[i, t], core_peer)
@@ -162,18 +166,31 @@
     def logits_across(i):
         a1(i).wait_recv()
         lzs[i] = lp[i, mine] + la[i]
-        if i == 0:
-            a2(i).start()
+        a2(i).start()
 
     def logits_whole(i):
         a2(i).wait_recv()
         lf[i, mine] = lzs[i] + lzr[i]
         a3(i, mine).start()
+
+    def send_along_z(i, t, rows):
+        for lanes in range(2):
+            fa[t, lanes] = rows[:, lanes * 128 : (lanes + 1) * 128]
+        for low in range(NZL):
+            rows = [fa[t, lanes, pl.ds(low, NJ, stride=8), :] for lanes in range(2)]
+            r2[i, t, low] = jnp.concatenate(rows, axis=1).astype(BF16)
+        each(along_z, lambda k: b2(i, t, z_at(k)).start())
+        if i:
+            x[t, h * NZL + zl] = r2[i, t, zl]
+        else:
+            wz[t, z] = r2[i, t, zl]
+
+    def send_slots(i, t, rows):
         if i == 0:
-            a2(1).start()
-
-    def send_slots(i, t):
-        each(in_plane, lambda d: b1(i, t, j_at(d), j, j_dev(j_at(d))).start())
+            send_along_z(i, t, rows)
+            return
+        s[i, t] = rows.reshape(NJ, 8, QF).astype(BF16)
+        each(in_plane, lambda d: b1(i, t, j_at(d), j_dev(j_at(d))).start())
         r1[i, t, j] = s[i, t, j]
 
     def dispatches(i):
@@ -186,8 +203,7 @@
         disp[i] = dispatch
         dispatch_low = dispatch.astype(BF16)
         dlow[i] = dispatch_low
-        s[i, 0] = dot(dispatch_low, tok[i], 0, 0).reshape(NJ, 8, QF).astype(BF16)
-        send_slots(i, 0)
+        send_slots(i, 0, dot(dispatch_low, tok[i], 0, 0))
 
     def combines(i):
         logits = lf[i]
@@ -198,8 +214,7 @@
         comb[i] = combine
         combine_low = combine.astype(BF16)
         clow[i] = combine_low
-        s[i, 1] = dot(combine_low, cot[i], 0, 0).reshape(NJ, 8, QF).astype(BF16)
-        send_slots(i, 1)
+        send_slots(i, 1, dot(combine_low, cot[i], 0, 0))
         total = top + jnp.log(below)
         tcomb[i] = (2.0 * loss_weight) * total * combine
         wide = jnp.broadcast_to(loss_weight * total * total, (TP, SLOTS))
@@ -207,17 +222,23 @@
 
     def to_experts(i, t):
         b1_all(i, t).wait_recv()
-        rows = r1[i, t].astype(F32).reshape(SLOTS, QF)
-        for lanes in range(2):
-            fa[t, lanes] = rows[:, lanes * 128 : (lanes + 1) * 128]
-        for low in range(NZL):
-            rows = [fa[t, lanes, pl.ds(low, NJ, stride=8), :] for lanes in range(2)]
-            r2[i, t, low] = jnp.concatenate(rows, axis=1).astype(BF16)
-        each(along_z, lambda k: b2(i, t, z_at(k)).start())
-        x[i, t, h * NZL + zl] = r2[i, t, zl]
+        send_along_z(i, t, r1[i, t].astype(F32).reshape(SLOTS, QF))
+
+    def cross(t):
+        b2_all(0, t).wait_recv()
+        for k in range(2):
+            rows = wz[t, k * NZL : (k + 1) * NZL].astype(F32).reshape(SLOTS, QF)
+            for lanes in range(2):
+                fw[k, lanes] = rows[:, lanes * 128 : (lanes + 1) * 128]
+        for dst in range(NJ):
+            for k in range(2):
+                rows = [fw[k, lanes, pl.ds(dst, 8, stride=NJ), :] for lanes in range(2)]
+                xs[t, dst, k] = jnp.concatenate(rows, axis=1).astype(BF16)
+        each(in_plane, lambda d: b1(0, t, j_at(d), j_dev(j_at(d))).start())
+        x0[t, 0, j] = xs[t, j]
 
     def arrive(i, t):
-        b2_all(i, t).wait_recv()
+        (b2_all if i else b1_all)(i, t).wait_recv()
         for half in range(2):
             fwd(i, t, half, c).start()
 
@@ -226,17 +247,21 @@
 
     FB = 256
 
-    def by_features(i, t, core, product):
-        arrived = [x[i, t, pl.ds((k * 2 + core) * NZL, NZL)].reshape(SLOTS, QF) for k in range(2)]
+    def by_features(i, t, side, product):
+        core = (1 - c) if side else c
+        if i == 0:
+            arrived = [x0[t, side, :, k].astype(F32).reshape(SLOTS, QF).astype(BF16) for k in range(2)]
+        else:
+            arrived = [x[t, pl.ds((k * 2 + core) * NZL, NZL)].reshape(SLOTS, QF) for k in range(2)]
         for f in range(0, 1024, FB):
             yield f, sum(product(arrived[k], quarter(k, core), f) for k in range(2))
 
     def project(i, t, product):
-        for f, total in by_features(i, t, c, product):
+        for f, total in by_features(i, t, 0, product):
             part[:, f : f + FB] = total
         for half in range(2):
             fwd(i, t, half, 1 - c).wait_recv()
-        for f, total in by_features(i, t, 1 - c, product):
+        for f, total in by_features(i, t, 1, product):
             yield f, part[:, f : f + FB] + total
 
     def expert_out(i):
@@ -267,9 +292,12 @@
             total = own[k] + px_r[i, t, k].astype(F32)
             if t == 0:
                 total = total + jnp.where(zh == k, 1.0, 0.0) * bo[...].astype(F32)
+            if i == 0:
+                cq[i, t, :, k] = total.reshape(NJ, 8, QF).astype(BF16)
+                continue
             for lanes in range(2):
                 ft[k, lanes] = total[:, lanes * 128 : (lanes + 1) * 128]
-        for dst in range(NJ):
+        for dst in range(NJ if i else 0):
             for k in range(2):
                 rows = [ft[k, lanes, pl.ds(dst, 8, stride=NJ), :] for lanes in range(2)]
                 cq[i, t, dst, k] = jnp.concatenate(rows, axis=1).astype(BF16)
@@ -337,13 +365,13 @@
     logits_whole(0)
     dispatches(0)
     combines(0)
-    to_experts(0, 0)
-    to_experts(0, 1)
     logits_whole(1)
     dispatches(1)
     combines(1)
+    cross(0)
     to_experts(1, 0)
     to_experts(1, 1)
+    cross(1)
     for load in loads[3:]:
         load.wait()
     arrive(0, 0)
@@ -420,7 +448,11 @@
         ((IMG, 2, NJ, 8, QF), BF16),
         ((2, 2, SLOTS, 128), F32),
         ((IMG, 2, NZL, NJ, QF), BF16),
-        ((IMG, 2, 4 * NZL, NJ, QF), BF16),
+        ((2, 4 * NZL, NJ, QF), BF16),
+        ((2, NZ, NJ, QF), BF16),
+        ((2, 2, SLOTS, 128), F32),
+        ((2, NJ, 2, 8, QF), BF16),
+        ((2, 2, NJ, 2, 8, QF), BF16),
         ((2, SLOTS, 1024), BF16),
         ((SLOTS, 1024), F32),
         ((SLOTS, 1024), F32),

time: 93.2 us -> 91.5 us (0.982)
  Pallas kernels: 92.4 us -> 90.8 us
    pallas_call x1, Pallas kernels: 91.1 us -> 89.5 us  [per_device(): pl.pallas_call(kernel, out_shape=(jax.ShapeDtypeStruct((IMG, TOK, QF), BF...]
where the time goes in v5:
time: 91.5 us; the launch traced here: 91.4 us
  Pallas kernels  90.8 us (99%)
    pallas_call x1, Pallas kernels, per_device(): pl.pallas_call(kernel, out_shape=(jax.ShapeDtypeStruct((IMG, TOK, QF), BF...  89.5 us

profile of v5, /device:TPU:1, one launch (start us, length us, event | category | flops | bytes accessed | tf_op | source)
XLA Modules:
  0.0 91.4 jit_solution(3824891297500126736)
XLA Ops:
  0.6 89.5 %layer.1 = (bf16[2,196,256]{2,1,0:T(8,128)(2,1)S(1)}, bf16[2,196,256]{2,1,0:T(8,128)(2,1)S(1)}, f32[2,196]{1,0:T(2,128)S(1)}) custom-call(bf16[196,2,256]{2,1,0:T(2,128)(2,1)} %bitcast.8, bf16[256,128]{1,0:T(8,128)(2,1)} %sp_hbm.1, bf16[1024,1024]{1,0:T(8,128)(2,1)} %bitcast.6, bf16[1,1024]{1,0:T(2,128)(2,1)} %bi_hbm.1, bf16[1024,1024]{1,0:T(8,128)(2,1)} %bitcast.7, ...), custom_call_target="tpu_custom_call" | custom-call | tf_op jit(solution)/shard_map/layer/pallas_call | solution.py:477
  90.1 1.3 %deliver.1 = (bf16[196,2,256]{2,1,0:T(2,128)(2,1)}, bf16[196,2,256]{2,1,0:T(2,128)(2,1)}, f32[2,196]{1,0:T(2,128)}) custom-call(bf16[2,196,256]{2,1,0:T(8,128)(2,1)S(1)} %get-tuple-element.9.mixed_in, bf16[2,196,256]{2,1,0:T(8,128)(2,1)S(1)} %get-tuple-element.10.tgrad_in, f32[2,196]{1,0:T(2,128)S(1)} %get-tuple-element.11.zloss_in), custom_call_target="tpu_custom_call" | custom-call | tf_op jit(solution)/shard_map/deliver/pallas_call | solution.py:505
